TPU v7x, 256 devices: a whole 4x4x8 slice. The times are simulated.
256 devices in a mesh: section: 64 (over y_hi, x, z), dp: 4 (over y_lo, core).
Axes of the slice: x: 4, y: 4 (y_hi: 2, y_lo: 2; y = y_hi * 2 + y_lo), z: 8, core: 2. Of those that a mesh axis runs over, the one named last changes fastest.
Arguments:
- streams: bfloat16 [2, 64, 4, 128, 1024], P(None, 'section', 'dp'), may hold values from -45 to 45
- cotangents: bfloat16 [2, 64, 4, 128, 1024], P(None, 'section', 'dp'), may hold values from -6 to 6
- weights: bfloat16 [64, 1024, 4096], P('section'), may hold values from -0.1875 to 0.1875
- norm_gains: float32 [64, 1024], P('section'), may hold values from 0.25 to 1.75
- segment_ids: int32 [64, 4, 128], P(None, 'dp'), may hold values from 0 to 1, never falling along the last dimension, each value on 1 to 96 neighbouring positions
Outputs:
- out_streams: bfloat16 [2, 64, 4, 128, 1024], P(None, 'section', 'dp')
- out_cotangents: bfloat16 [2, 64, 4, 128, 1024], P(None, 'section', 'dp')
- weight_grads: bfloat16 [64, 1024, 4096], P('section', 'dp')
- gain_grads: float32 [64, 1024], P('section', 'dp')
Inputs may be any that keep to these rules, and one draw needn't show every extreme that they name: `segment_ids`: along each row of 128 tokens the document numbers never fall; each row is a 128-token window of packed documents, attention stays inside the window, and each document has 1 to 96 tokens in it.
All inputs are finite; a program needn't handle non-finite values.
Results may differ from a plain program's by a relative error of at most 0.018.
Values may be sent and summed in bfloat16 or wider, within the bound.
No kernel may reach another device: no remote copies, remote signals or barrier semaphores. Data moves between devices by JAX's collectives and lax.ppermute only.
A program may use at most 128 MiB of HBM per device.

v0:
```python
from functools import partial
import math

import jax
import jax.numpy as jnp
from jax import lax
from jax.experimental import pallas as pl
from jax.experimental.pallas import tpu as pltpu
from jax.sharding import PartitionSpec as P


D = 1024
FF = 2048
TICKS = 3
CHUNK = 512
CHUNKS = 4 * D // CHUNK
PAIR = 128
UNROLL = 2
RELAYS = {"p2": 1, "a": 2, "c": 3}
QUARTER = D // 4

epsilon = 1e-05
bf16 = jnp.bfloat16
f32 = jnp.float32

NN = (((1,), (0,)), ((), ()))
NT = (((1,), (1,)), ((), ()))
TN = (((0,), (0,)), ((), ()))


def dot(first, second, dims=NN):
    return lax.dot_general(first, second, dims, preferred_element_type=f32)


def cols(index, width):
    start = index * width
    return pl.ds(start if isinstance(start, int) else pl.multiple_of(start, width), width)


def add_terms(acc_ref, rows_ref, w_ref, count, offset):
    acc_ref[...] = dot(rows_ref[:, cols(0, CHUNK)], w_ref[:, cols(offset, CHUNK)], NT)

    def step(chunk, carry):
        acc_ref[...] += dot(rows_ref[:, cols(chunk, CHUNK)], w_ref[:, cols(chunk + offset, CHUNK)], NT)
        return carry

    lax.fori_loop(1, count, step, 0)


def weight_copies(w_hbm, w_ref, sems, order):
    copies = {}
    for chunk in order:
        piece = cols(chunk, CHUNK)
        copies[chunk] = pltpu.make_async_copy(
            w_hbm.at[:, piece], w_ref.at[:, piece], sems.at[chunk]
        )
    for chunk in order:
        copies[chunk].start()
    return copies


def low_lanes(rows):
    return lax.broadcasted_iota(jnp.int32, (rows, PAIR), 1) < 64


def half_sums(values, low):
    first = jnp.sum(jnp.where(low, values, 0.0), axis=-1, keepdims=True)
    second = jnp.sum(jnp.where(low, 0.0, values), axis=-1, keepdims=True)
    return first, second


def attention_mask(anchor, seg_ref):
    rows = seg_ref.shape[1]
    segment = seg_ref[pl.ds(anchor, 1), :].astype(f32)
    across = jnp.broadcast_to(segment, (rows, rows))
    down = across.T
    row_index = lax.broadcasted_iota(jnp.int32, (rows, rows), 0)
    col_index = lax.broadcasted_iota(jnp.int32, (rows, rows), 1)
    allowed = (across == down) & (col_index <= row_index)
    mask = jnp.where(allowed, 1.0, 0.0)
    return jnp.concatenate([mask, mask], axis=0)


def split_pair(values, low_b, high_b):
    return jnp.concatenate([values * low_b, values * high_b], axis=0)


def pair_weights(q_ref, k_ref, lane, mask, low_b, high_b):
    q_split = split_pair(q_ref[:, lane], low_b, high_b)
    k = k_ref[:, lane]
    scores = dot(q_split, k, NT) * 0.125
    raised = jnp.exp(scores) * mask
    total = jnp.sum(raised, axis=-1, keepdims=True)
    return q_split, k, raised / total


GELU_A = math.sqrt(2.0 / math.pi)
GELU_B = 0.044715


class Ready:
    def wait(self):
        pass


RESIDENT = (Ready(),) * CHUNKS


def first_forward_kernel(tick, info_ref, y1_ref, y2_ref, g_ref, seg_ref, w_hbm,
                         a_ref, n_ref, x2_ref, s1_ref, s2_ref, w_ref, acc_ref, sems):
    copies = weight_copies(w_hbm, w_ref, sems, range(CHUNKS))
    forward_body(copies, tick, info_ref, y1_ref, y2_ref, g_ref, seg_ref, w_ref,
                 a_ref, n_ref, x2_ref, s1_ref, s2_ref, acc_ref)


def forward_kernel(tick, *refs):
    forward_body(RESIDENT, tick, *refs)


def forward_body(copies, tick, info_ref, y1_ref, y2_ref, g_ref, seg_ref, w_ref,
                 a_ref, n_ref, x2_ref, s1_ref, s2_ref, acc_ref):
    rows = y1_ref.shape[0]
    stream = y1_ref[...].astype(f32)
    mean_square = jnp.mean(stream * stream, axis=-1, keepdims=True)
    n_ref[...] = (stream * lax.rsqrt(mean_square + epsilon) * g_ref[...]).astype(bf16)

    @pl.when(info_ref[0] == 0)
    def _():
        low = low_lanes(rows)
        low_b = jnp.where(low, 1.0, 0.0).astype(bf16)
        high_b = jnp.where(low, 0.0, 1.0).astype(bf16)
        for chunk in range(6):
            copies[chunk].wait()
            projected = dot(n_ref[...], w_ref[:, cols(chunk, CHUNK)])
            for inner in range(CHUNK // PAIR):
                part = projected[:, inner * PAIR:(inner + 1) * PAIR]
                pair = chunk * (CHUNK // PAIR) + inner
                if chunk < 4:
                    first, second = half_sums(part * part, low)
                    r_first = lax.rsqrt(first * (1.0 / 64) + epsilon)
                    r_second = lax.rsqrt(second * (1.0 / 64) + epsilon)
                    scale = jnp.where(low, r_first, r_second)
                    s1_ref[:, cols(pair, PAIR)] = scale
                    part = part * scale
                s2_ref[:, cols(pair, PAIR)] = part.astype(bf16)
        mask = attention_mask(info_ref[3 + tick], seg_ref)
        for pair in range(8):
            _, _, weights = pair_weights(
                s2_ref.at[:, :D], s2_ref.at[:, D:2 * D], cols(pair, PAIR), mask, low_b, high_b
            )
            soft = weights.astype(bf16)
            v = s2_ref[:, cols(16 + pair, PAIR)]
            mixed = dot(soft[:rows], v * low_b) + dot(soft[rows:], v * high_b)
            x2_ref[:, cols(pair, PAIR)] = mixed.astype(bf16)
        for chunk in (6, 7):
            copies[chunk].wait()
            out = cols(chunk - 6, CHUNK)
            branch = dot(x2_ref[:, :D], w_ref[:, cols(chunk, CHUNK)])
            a_ref[:, out] = (y2_ref[:, out].astype(f32) - branch).astype(bf16)

    @pl.when(info_ref[0] == 1)
    def _():
        def hidden_step(chunk, carry):
            piece = cols(chunk, CHUNK)
            pre = dot(n_ref[...], w_ref[:, piece])
            square = pre * pre
            bend = jnp.tanh(GELU_A * (pre + GELU_B * (pre * square)))
            half = 0.5 * (1.0 + bend)
            x2_ref[:, piece] = (pre * half).astype(bf16)
            slope = GELU_A * (1.0 + (3.0 * GELU_B) * square)
            s1_ref[:, piece] = half + 0.5 * pre * (1.0 - bend * bend) * slope
            return carry

        if copies is RESIDENT:
            lax.fori_loop(0, 4, hidden_step, 0)
            add_terms(acc_ref, x2_ref, w_ref, 4, 4)
        else:
            for chunk in range(4):
                copies[chunk].wait()
                hidden_step(chunk, 0)
            for chunk in range(4, 8):
                copies[chunk].wait()
            add_terms(acc_ref, x2_ref, w_ref, 4, 4)
        a_ref[...] = (y2_ref[...].astype(f32) - acc_ref[...]).astype(bf16)


def first_backward_kernel(tick, *refs):
    backward_kernel(tick, *refs[:6], None, *refs[6:])


def backward_kernel(tick, info_ref, y1_ref, c1_ref, c2_ref, g_ref, seg_ref, dg_in_ref,
                    n_ref, x2_ref, s1_ref, s2_ref, w_ref,
                    c_ref, right_ref, keep_ref, send_ref, dg_ref, acc_ref):
    rows = y1_ref.shape[0]
    chip, core = info_ref[1], info_ref[2]
    blocks = (2 * chip + core, 2 * (1 - chip) + core)
    other = (2 * chip + 1 - core, 2 * (1 - chip) + 1 - core)

    def spread(left, half):
        for place, (mine, theirs) in enumerate(zip(blocks, other)):
            out = cols(2 * half + place, QUARTER)
            keep_ref[:, out] = left[:, pl.ds(pl.multiple_of(mine * QUARTER, QUARTER), QUARTER)]
            send_ref[:, out] = left[:, pl.ds(pl.multiple_of(theirs * QUARTER, QUARTER), QUARTER)]

    spread(n_ref, 0)

    @pl.when(info_ref[0] == 0)
    def _():
        spread(x2_ref, 1)
        right_ref[:, 3 * D:] = c2_ref[...]
        low = low_lanes(rows)
        low_b = jnp.where(low, 1.0, 0.0).astype(bf16)
        high_b = jnp.where(low, 0.0, 1.0).astype(bf16)
        mask = attention_mask(info_ref[3 + tick], seg_ref)
        add_terms(acc_ref, c2_ref, w_ref, 2, 6)

        def norm_back(dy, y_b, pair):
            dy = dy.astype(bf16).astype(f32)
            y = y_b.astype(f32)
            first, second = half_sums(dy * y, low)
            mean = jnp.where(low, first, second) * (1.0 / 64)
            return (s1_ref[:, cols(pair, PAIR)] * (dy - y * mean)).astype(bf16)

        def pair_back(pair):
            lane = cols(pair, PAIR)
            q_split, k, weights = pair_weights(
                s2_ref.at[:, :D], s2_ref.at[:, D:2 * D], lane, mask, low_b, high_b
            )
            soft = weights.astype(bf16)
            v = s2_ref[:, cols(16 + pair, PAIR)]
            d_mix = split_pair(acc_ref[:, lane].astype(bf16), low_b, high_b)
            d_soft = dot(d_mix, v, NT).astype(bf16).astype(f32)
            dv = dot(soft, d_mix, TN)
            product = d_soft * weights
            d_scores = (product - weights * jnp.sum(product, axis=-1, keepdims=True)) * 0.125
            d_scores = d_scores.astype(bf16)
            dq = dot(d_scores[:rows], k * low_b) + dot(d_scores[rows:], k * high_b)
            dk = dot(d_scores, q_split, TN)
            right_ref[:, lane] = norm_back(dq, s2_ref[:, lane], pair)
            right_ref[:, cols(8 + pair, PAIR)] = norm_back(dk, k, 8 + pair)
            right_ref[:, cols(16 + pair, PAIR)] = dv.astype(bf16)

        def pair_step(step, carry):
            for inner in range(UNROLL):
                pair_back(step * UNROLL + inner)
            return carry

        lax.fori_loop(0, 8 // UNROLL, pair_step, 0)
        add_terms(acc_ref, right_ref, w_ref, 6, 0)

    @pl.when(info_ref[0] == 1)
    def _():
        spread(c2_ref, 1)
        right_ref[:, FF:] = x2_ref[...]

        def hidden_step(chunk, carry):
            piece = cols(chunk, CHUNK)
            grad = dot(c2_ref[...], w_ref[:, cols(chunk + 4, CHUNK)])
            right_ref[:, piece] = (grad * s1_ref[:, piece]).astype(bf16)
            return carry

        lax.fori_loop(0, 4, hidden_step, 0)
        add_terms(acc_ref, right_ref, w_ref, 4, 0)

    stream = y1_ref[...].astype(f32)
    inverse = lax.rsqrt(jnp.mean(stream * stream, axis=-1, keepdims=True) + epsilon)
    unit = stream * inverse
    grad_normed = acc_ref[...]
    dg = jnp.sum(grad_normed * unit, axis=0, keepdims=True)
    dg_ref[...] = dg if dg_in_ref is None else dg_in_ref[...] + dg
    scaled = grad_normed * g_ref[...]
    du = inverse * (scaled - unit * jnp.mean(scaled * unit, axis=-1, keepdims=True))
    c_ref[...] = (c1_ref[...].astype(f32) + du).astype(bf16)


def vmem():
    return pl.BlockSpec(memory_space=pltpu.VMEM)


def smem():
    return pl.BlockSpec(memory_space=pltpu.SMEM)


def hbm():
    return pl.BlockSpec(memory_space=pltpu.HBM)


def held(value):
    return pltpu.with_memory_space_constraint(value, pltpu.VMEM)


def shape(dims, dtype=bf16):
    return jax.ShapeDtypeStruct(dims, dtype)


MIB = 1 << 20


def forward(tick, info, y1, y2, gain, segments, weight):
    rows = y1.shape[0]
    first = tick == 0
    fixed = pltpu.with_memory_space_constraint(weight, pltpu.HBM) if first else None
    saved = (
        pltpu.VMEM((rows, D), bf16), pltpu.VMEM((rows, FF), bf16),
        pltpu.VMEM((rows, FF), f32), pltpu.VMEM((rows, 3 * D), bf16),
    )
    scratch = [pltpu.VMEM((rows, D), f32)]
    resident = ()
    if first:
        resident = (pltpu.VMEM((D, 4 * D), bf16),)
        scratch.append(pltpu.SemaphoreType.DMA((CHUNKS,)))
    return pl.pallas_call(
        partial(first_forward_kernel if first else forward_kernel, tick),
        out_shape=(shape((rows, D)),) + saved + resident,
        in_specs=[smem()] + [vmem()] * 4 + [hbm() if first else vmem()],
        out_specs=(vmem(),) * (5 + len(resident)),
        scratch_shapes=scratch,
        compiler_params=pltpu.CompilerParams(vmem_limit_bytes=16 * MIB),
        cost_estimate=pl.CostEstimate(
            flops=8 * rows * D * D, bytes_accessed=12 * MIB, transcendentals=rows * FF
        ),
        name="tick_forward",
    )(info, y1, y2, gain, segments, fixed if first else held(weight))


def backward(tick, info, y1, c1, c2, gain, segments, dg, saved, weight):
    rows = y1.shape[0]
    carried = [] if tick == 0 else [dg]
    return pl.pallas_call(
        partial(first_backward_kernel if tick == 0 else backward_kernel, tick),
        out_shape=(
            shape((rows, D)), shape((rows, 4 * D)), shape((rows, D)),
            shape((rows, D)), shape((1, D), f32),
        ),
        in_specs=[smem()] + [vmem()] * (10 + len(carried)),
        out_specs=(vmem(),) * 5,
        scratch_shapes=[pltpu.VMEM((rows, D), f32)],
        compiler_params=pltpu.CompilerParams(vmem_limit_bytes=16 * MIB),
        cost_estimate=pl.CostEstimate(
            flops=8 * rows * D * D, bytes_accessed=12 * MIB, transcendentals=rows * FF
        ),
        name="tick_backward",
    )(info, y1, c1, c2, gain, segments, *carried, *saved, held(weight))


def grad_kernel(place, info_ref, *refs):
    count = 2 * TICKS
    lefts, rights, out_ref, turned_ref = refs[:count], refs[count:2 * count], refs[-2], refs[-1]
    rows = lefts[0].shape[0]
    for index, left in enumerate(lefts):
        for half in range(2):
            block = left[:, cols(2 * half + place, QUARTER)]
            turned_ref[half, :, cols(index, rows)] = block.T
    split = jnp.where(info_ref[0] == 0, 3 * D // CHUNK, FF // CHUNK)

    def step(chunk, carry):
        half = jnp.where(chunk >= split, 1, 0)
        piece = pl.ds(pl.multiple_of(chunk * CHUNK, CHUNK), CHUNK)
        right = jnp.concatenate([ref[:, piece] for ref in rights], axis=0)
        out_ref[:, piece] = dot(turned_ref[half], right).astype(out_ref.dtype)
        return carry

    lax.fori_loop(0, CHUNKS, step, 0)


def grad_block(info, lefts, rights, place, dtype):
    rows = lefts[0].shape[0]
    count = len(lefts)
    return pl.pallas_call(
        partial(grad_kernel, place),
        out_shape=shape((QUARTER, 4 * D), dtype),
        in_specs=[smem()] + [vmem()] * (2 * count),
        out_specs=vmem(),
        scratch_shapes=[pltpu.VMEM((2, QUARTER, count * rows), bf16)],
        compiler_params=pltpu.CompilerParams(vmem_limit_bytes=20 * MIB),
        cost_estimate=pl.CostEstimate(
            flops=2 * count * rows * D * D, bytes_accessed=10 * MIB, transcendentals=0
        ),
        name="grad_own" if place == 0 else "grad_other",
    )(info, *map(held, lefts), *map(held, rights))


def shards(streams, cotangents, weights, norm_gains, segment_ids):
    section = lax.axis_index("section")
    replica = lax.axis_index("dp")
    sections = lax.axis_size("section")
    replicas = lax.axis_size("dp")
    weight = weights[0]
    rows = streams.shape[3]
    segments = segment_ids[:, 0]
    ring = [(s, (s - 1) % sections) for s in range(sections)]

    def pass_on(value):
        return lax.ppermute(value, "section", ring)

    half = sections // 2

    def pass_relayed(value, column):
        direct = [(s, s - 1) for s in range(sections) if s % half]
        up = [(0, half + column), (half, column)]
        down = [(half + column, sections - 1), (column, half - 1)]
        lifted = lax.ppermute(value, "section", up)
        near = lax.ppermute(value, "section", direct)
        far = lax.ppermute(lifted, "section", down)
        return jnp.where(section % half == half - 1, far, near)

    def send(name, value, tick):
        if tick == TICKS - 1 and name in RELAYS:
            return pass_relayed(value, RELAYS[name] * half // 4)
        return pass_on(value)

    def exchange(value, bits):
        return lax.ppermute(value, "dp", [(r, r ^ bits) for r in range(replicas)])

    y1, y2 = streams[0, 0, 0], streams[1, 0, 0]
    c1, c2 = cotangents[0, 0, 0], cotangents[1, 0, 0]
    anchors = [(section + tick) % sections for tick in range(TICKS)]
    info = jnp.stack([section % 2, replica // 2, replica % 2] + anchors).astype(jnp.int32)
    dg = None
    lefts, rights = [], []
    for tick in range(TICKS):
        next_y2 = send("p1", y1, tick)
        next_c1 = send("p2", c2, tick)
        a, *saved = forward(tick, info, y1, y2, norm_gains, segments, weight)
        if tick == 0:
            weight = saved.pop()
        next_y1 = send("a", a, tick)
        c, right, keep, give, dg = backward(
            tick, info, y1, c1, c2, norm_gains, segments, dg, saved, weight
        )
        next_c2 = send("c", c, tick)
        lefts += [keep, exchange(give, 1)]
        rights += [right, exchange(right, 1)]
        y1, y2, c1, c2 = next_y1, next_y2, next_c1, next_c2
    dg_all = dg + exchange(dg, 1) + exchange(dg, 2) + exchange(dg, 3)
    grad_other = grad_block(info, lefts, rights, 1, bf16)
    received = exchange(grad_other, 2)
    grad_own = grad_block(info, lefts, rights, 0, f32)
    grad_scale = 1.0 / math.sqrt(TICKS * rows * replicas)
    weight_grads = ((grad_own + received.astype(f32)) * grad_scale).astype(bf16)[None]
    gain_grads = lax.dynamic_slice_in_dim(dg_all, replica * QUARTER, QUARTER, 1) * grad_scale
    out_streams = jnp.stack([y1, y2])[:, None, None]
    out_cotangents = jnp.stack([c1, c2])[:, None, None]
    return (out_streams, out_cotangents, weight_grads, gain_grads)


def solution(mesh):
    placed = (
        P(None, "section", "dp", None, None),
        P(None, "section", "dp", None, None),
        P("section", None, None),
        P("section", None),
        P(None, "dp", None),
    )
    return jax.shard_map(
        shards,
        mesh=mesh,
        in_specs=placed,
        out_specs=(
            P(None, "section", "dp", None, None),
            P(None, "section", "dp", None, None),
            P("section", "dp", None),
            P("section", "dp"),
        ),
        check_vma=False,
    )
```

profile of v0, /device:TPU:6, one launch (start us, length us, event | category | flops | bytes accessed | tf_op | source)
XLA Modules:
  0.0 171.4 jit_solution(3211819138706908594)
XLA Ops:
  0.6 1.3 slice_bitcast_fusion.1
  1.9 6.2 %collective-permute-start.1 = (bf16[128,1024]{1,0:T(8,128)(2,1)S(1)}, bf16[128,1024]{1,0:T(8,128)(2,1)S(1)}, u32[]{:S(2)}, u32[]{:S(2)}) collective-permute-start(bf16[128,1024]{1,0:T(8,128)(2,1)S(1)} %get-tuple-element.74.y1_ref.refs_1_), channel_id=1, source_target_pairs={{0,252},{4,0},{8,4},{12,8},{16,12},{20,16},{24,20},{28,24},{32,28}... | collective-permute-start | bytes 786440 | tf_op jit(solution)/shard_map/ppermute | solution.py:394
  8.2 0.8 copy-done.6
  8.9 0.7 copy-done.19
  9.6 5.7 %tick_forward.3 = (bf16[128,1024]{1,0:T(8,128)(2,1)S(1)}, bf16[128,1024]{1,0:T(8,128)(2,1)S(1)}, bf16[128,2048]{1,0:T(8,128)(2,1)S(1)}, f32[128,2048]{1,0:T(8,12...) custom-call(s32[6]{0:T(128)S(1)} %stack.45.info_ref.refs_0_, ...), custom_call_target="tpu_custom_call" | custom-call | flops 1073741824 | bytes 12582912 | tf_op jit(solution)/shard_map/tick_forward/pallas_call | solution.py:312
  15.3 1.5 collective-permute-start
  16.8 8.9 %tick_backward.3 = (bf16[128,1024]{1,0:T(8,128)(2,1)S(1)}, bf16[128,4096]{1,0:T(8,128)(2,1)S(1)}, bf16[128,1024]{1,0:T(8,128)(2,1)S(1)}, bf16[128,1024]{1,0:T(8,128)(2,1)S(1)}, f32[1,1024]{1,0:T(1,128)S(1)}) custom-call(s32[6]{0:T(128)S(1)} %stack.45.info_ref.refs_0_, bf16[128,1024]{1,0:T(8,128)(2,1)S(1)} %get-tuple-element.74.y1_ref.refs_1_, ...), custom_call_target="tpu_custom_call" | custom-call | flops 1073741824 | bytes 12582912 | tf_op jit(solution)/shard_map/tick_backward/pallas_call | solution.py:329
  25.8 2.0 %collective-permute-start.8 = (bf16[128,1024]{1,0:T(8,128)(2,1)S(1)}, bf16[128,1024]{1,0:T(8,128)(2,1)S(1)}, u32[]{:S(2)}, u32[]{:S(2)}) collective-permute-start(bf16[128,1024]{1,0:T(8,128)(2,1)S(1)} %get-tuple-element.70.refs_3_), channel_id=1, source_target_pairs={{0,252},{4,0},{8,4},{12,8},{16,12},{20,16},{24,20},{28,24},{32,28}... | collective-permute-start | bytes 786440 | tf_op jit(solution)/shard_map/ppermute | solution.py:394
  27.8 2.9 %tick_forward.4 = (bf16[128,1024]{1,0:T(8,128)(2,1)S(1)}, bf16[128,1024]{1,0:T(8,128)(2,1)S(1)}, bf16[128,2048]{1,0:T(8,128)(2,1)S(1)}, f32[128,2048]{1,0:T(8,128)S(1)}, bf16[128,3072]{1,0:T(8,128)(2,1)S(1)}) custom-call(s32[6]{0:T(128)S(1)} %stack.45.info_ref.refs_0_, bf16[128,1024]{1,0:T(8,128)(2,1)S(1)} %collective-permute-done.refs_1_.y1_ref, ...), custom_call_target="tpu_custom_call" | custom-call | flops 1073741824 | bytes 12582912 | tf_op jit(solution)/shard_map/tick_forward/pallas_call | solution.py:312
  30.7 1.9 %collective-permute-start.2 = (bf16[128,1024]{1,0:T(8,128)(2,1)S(1)}, bf16[128,1024]{1,0:T(8,128)(2,1)S(1)}, u32[]{:S(2)}, u32[]{:S(2)}) collective-permute-start(bf16[128,1024]{1,0:T(8,128)(2,1)S(1)} %get-tuple-element.37), channel_id=1, source_target_pairs={{0,252},{4,0},{8,4},{12,8},{16,12},{20,16},{24,20},{28,24},{32,28}... | collective-permute-start | bytes 786440 | tf_op jit(solution)/shard_map/ppermute | solution.py:394
  32.7 2.2 %collective-permute-done.9.c2_ref = bf16[128,1024]{1,0:T(8,128)(2,1)S(1)} collective-permute-done((bf16[128,1024]{1,0:T(8,128)(2,1)S(1)}, bf16[128,1024]{1,0:T(8,128)(2,1)S(1)}, u32[]{:S(2)}, u32[]{:S(2)}) %collective-permute-start.9) | collective-permute-done | bytes 262176 | tf_op jit(solution)/shard_map/ppermute | solution.py:394
  34.9 5.6 %collective-permute-done.8.c1_ref = bf16[128,1024]{1,0:T(8,128)(2,1)S(1)} collective-permute-done((bf16[128,1024]{1,0:T(8,128)(2,1)S(1)}, bf16[128,1024]{1,0:T(8,128)(2,1)S(1)}, u32[]{:S(2)}, u32[]{:S(2)}) %collective-permute-start.8) | collective-permute-done | bytes 262176 | tf_op jit(solution)/shard_map/ppermute | solution.py:394
  40.5 8.9 %tick_backward.4 = (bf16[128,1024]{1,0:T(8,128)(2,1)S(1)}, bf16[128,4096]{1,0:T(8,128)(2,1)S(1)}, bf16[128,1024]{1,0:T(8,128)(2,1)S(1)}, bf16[128,1024]{1,0:T(8,128)(2,1)S(1)}, f32[1,1024]{1,0:T(1,128)S(1)}) custom-call(s32[6]{0:T(128)S(1)} %stack.45.info_ref.refs_0_, bf16[128,1024]{1,0:T(8,128)(2,1)S(1)} %collective-permute-done.refs_1_.y1_ref, ...), custom_call_target="tpu_custom_call" | custom-call | flops 1073741824 | bytes 12582912 | tf_op jit(solution)/shard_map/tick_backward/pallas_call | solution.py:329
  49.5 2.0 %collective-permute-start.14 = (bf16[128,1024]{1,0:T(8,128)(2,1)S(1)}, bf16[128,1024]{1,0:T(8,128)(2,1)S(1)}, u32[]{:S(2)}, u32[]{:S(2)}) collective-permute-start(bf16[128,1024]{1,0:T(8,128)(2,1)S(1)} %collective-permute-done.9.c2_ref), channel_id=1, source_target_pairs={{0,252},{4,0},{8,4},{12,8},{16,12},{20,16},{24,20},{28,24},{32,28}... | collective-permute-start | bytes 786440 | tf_op jit(solution)/shard_map/ppermute | solution.py:394
  51.5 0.5 collective-permute-start.22
  52.0 3.0 %tick_forward.5 = (bf16[128,1024]{1,0:T(8,128)(2,1)S(1)}, bf16[128,1024]{1,0:T(8,128)(2,1)S(1)}, bf16[128,2048]{1,0:T(8,128)(2,1)S(1)}, f32[128,2048]{1,0:T(8,128)S(1)}, bf16[128,3072]{1,0:T(8,128)(2,1)S(1)}) custom-call(s32[6]{0:T(128)S(1)} %stack.45.info_ref.refs_0_, bf16[128,1024]{1,0:T(8,128)(2,1)S(1)} %collective-permute-done.2.refs_1_.y1_ref, ...), custom_call_target="tpu_custom_call" | custom-call | flops 1073741824 | bytes 12582912 | tf_op jit(solution)/shard_map/tick_forward/pallas_call | solution.py:312
  55.0 0.7 copy-done.21
  55.7 2.9 %collective-permute-done.10.c2_ref = bf16[128,1024]{1,0:T(8,128)(2,1)} collective-permute-done((bf16[128,1024]{1,0:T(8,128)(2,1)S(1)}, bf16[128,1024]{1,0:T(8,128)(2,1)}, u32[]{:S(2)}, u32[]{:S(2)}) %collective-permute-start.10) | collective-permute-done | bytes 262176 | tf_op jit(solution)/shard_map/ppermute | solution.py:394
  58.6 2.7 %collective-permute-done.14.c1_ref = bf16[128,1024]{1,0:T(8,128)(2,1)S(1)} collective-permute-done((bf16[128,1024]{1,0:T(8,128)(2,1)S(1)}, bf16[128,1024]{1,0:T(8,128)(2,1)S(1)}, u32[]{:S(2)}, u32[]{:S(2)}) %collective-permute-start.14) | collective-permute-done | bytes 262176 | tf_op jit(solution)/shard_map/ppermute | solution.py:394
  61.3 10.0 %tick_backward.5 = (bf16[128,1024]{1,0:T(8,128)(2,1)}, bf16[128,4096]{1,0:T(8,128)(2,1)S(1)}, bf16[128,1024]{1,0:T(8,128)(2,1)S(1)}, bf16[128,1024]{1,0:T(8,128)(2,1)S(1)}, f32[1,1024]{1,0:T(1,128)S(1)}) custom-call(s32[6]{0:T(128)S(1)} %stack.45.info_ref.refs_0_, bf16[128,1024]{1,0:T(8,128)(2,1)S(1)} %collective-permute-done.2.refs_1_.y1_ref, ...), custom_call_target="tpu_custom_call" | custom-call | flops 1073741824 | bytes 12582912 | tf_op jit(solution)/shard_map/tick_backward/pallas_call | solution.py:329
  71.3 0.5 collective-permute-start.18
  71.9 2.4 %collective-permute-done.18.refs_1_ = bf16[128,1024]{1,0:T(8,128)(2,1)S(1)} collective-permute-done((bf16[128,1024]{1,0:T(8,128)(2,1)S(1)}, bf16[128,1024]{1,0:T(8,128)(2,1)S(1)}, u32[]{:S(2)}, u32[]{:S(2)}) %collective-permute-start.18) | collective-permute-done | bytes 262176 | tf_op jit(solution)/shard_map/ppermute | solution.py:413
  74.7 1.2 collective-permute-done.20.refs_5_
  76.0 5.1 %grad_other.1 = bf16[256,4096]{1,0:T(8,128)(2,1)} custom-call(s32[6]{0:T(128)S(1)} %stack.45.info_ref.refs_0_, bf16[128,1024]{1,0:T(8,128)(2,1)S(1)} %get-tuple-element.56.refs_0_, bf16[128,1024]{1,0:T(8,128)(2,1)S(1)} %collective-permute-done.18.refs_1_, bf16[128,1024]{1,0:T(8,128)(2,1)S(1)} %get-tuple-element.58.refs_2_, ...), custom_call_target="tpu_custom_call" | custom-call | flops 1610612736 | bytes 10485760 | tf_op jit(solution)/shard_map/grad_other/pallas_call | solution.py:369
  81.1 1.7 collective-permute-start.24
  82.8 1.4 collective-permute-start.11
  84.2 1.9 %collective-permute-start.13 = (bf16[128,1024]{1,0:T(8,128)(2,1)}, bf16[128,1024]{1,0:T(8,128)(2,1)}, u32[]{:S(2)}, u32[]{:S(2)}) collective-permute-start(bf16[128,1024]{1,0:T(8,128)(2,1)} %collective-permute-done.10.c2_ref), channel_id=1, source_target_pairs={{4,0},{8,4},{12,8},{16,12},{20,16},{24,20},{28,24},{32,28},{36,32}... | collective-permute-start | bytes 786440 | tf_op jit(solution)/shard_map/ppermute | solution.py:403
  86.1 1.3 collective-permute-start.15
  87.4 1.4 collective-permute-start.12
  88.8 1.2 collective-permute-done.25
  90.4 44.4 %collective-permute-done.26 = f32[1,1024]{1,0:T(1,128)S(1)} collective-permute-done((f32[1,1024]{1,0:T(1,128)S(1)}, f32[1,1024]{1,0:T(1,128)S(1)}, u32[]{:S(2)}, u32[]{:S(2)}) %collective-permute-start.26) | collective-permute-done | bytes 4128 | tf_op jit(solution)/shard_map/ppermute | solution.py:413
  134.9 0.5 collective-permute-start.27
  135.4 2.5 %collective-permute-done.27 = f32[1,1024]{1,0:T(1,128)S(1)} collective-permute-done((f32[1,1024]{1,0:T(1,128)S(1)}, f32[1,1024]{1,0:T(1,128)S(1)}, u32[]{:S(2)}, u32[]{:S(2)}) %collective-permute-start.27) | collective-permute-done | bytes 4128 | tf_op jit(solution)/shard_map/ppermute | solution.py:413
  137.9 1.9 %collective-permute-start.17 = (bf16[128,1024]{1,0:T(8,128)(2,1)}, bf16[128,1024]{1,0:T(8,128)(2,1)S(1)}, u32[]{:S(2)}, u32[]{:S(2)}) collective-permute-start(bf16[128,1024]{1,0:T(8,128)(2,1)} %get-tuple-element.55), channel_id=1, source_target_pairs={{4,0},{8,4},{12,8},{16,12},{20,16},{24,20},{28,24},{32,28},{36,32}... | collective-permute-start | bytes 786440 | tf_op jit(solution)/shard_map/ppermute | solution.py:403
  139.8 0.7 collective-permute-start.4
  140.5 1.3 collective-permute-start.16
  141.8 0.6 fusion.1
  142.4 1.9 %collective-permute-start.6 = (bf16[128,1024]{1,0:T(8,128)(2,1)}, bf16[128,1024]{1,0:T(8,128)(2,1)S(1)}, u32[]{:S(2)}, u32[]{:S(2)}) collective-permute-start(bf16[128,1024]{1,0:T(8,128)(2,1)} %copy-done.21), channel_id=1, source_target_pairs={{4,0},{8,4},{12,8},{16,12},{20,16},{24,20},{28,24},{32,28},{36,32}... | collective-permute-start | bytes 786440 | tf_op jit(solution)/shard_map/ppermute | solution.py:403
  144.3 1.0 select_bitcast_fusion.1
  145.3 3.8 %collective-permute-done.17 = bf16[128,1024]{1,0:T(8,128)(2,1)S(1)} collective-permute-done((bf16[128,1024]{1,0:T(8,128)(2,1)}, bf16[128,1024]{1,0:T(8,128)(2,1)S(1)}, u32[]{:S(2)}, u32[]{:S(2)}) %collective-permute-start.17) | collective-permute-done | bytes 262176 | tf_op jit(solution)/shard_map/ppermute | solution.py:403
  149.2 2.1 %collective-permute-start.7 = (bf16[128,1024]{1,0:T(8,128)(2,1)}, bf16[128,1024]{1,0:T(8,128)(2,1)S(1)}, u32[]{:S(2)}, u32[]{:S(2)}) collective-permute-start(bf16[128,1024]{1,0:T(8,128)(2,1)} %copy-done.18), channel_id=1, source_target_pairs={{0,252},{4,0},{8,4},{12,8},{16,12},{20,16},{24,20},{28,24},{32,28}... | collective-permute-start | bytes 786440 | tf_op jit(solution)/shard_map/ppermute | solution.py:394
  151.3 0.7 collective-permute-start.5
  152.4 0.8 maximum_bitcast_fusion.1
  153.3 4.7 %collective-permute-done.6 = bf16[128,1024]{1,0:T(8,128)(2,1)S(1)} collective-permute-done((bf16[128,1024]{1,0:T(8,128)(2,1)}, bf16[128,1024]{1,0:T(8,128)(2,1)S(1)}, u32[]{:S(2)}, u32[]{:S(2)}) %collective-permute-start.6) | collective-permute-done | bytes 262176 | tf_op jit(solution)/shard_map/ppermute | solution.py:403
  158.1 5.0 %collective-permute-done.7 = bf16[128,1024]{1,0:T(8,128)(2,1)S(1)} collective-permute-done((bf16[128,1024]{1,0:T(8,128)(2,1)}, bf16[128,1024]{1,0:T(8,128)(2,1)S(1)}, u32[]{:S(2)}, u32[]{:S(2)}) %collective-permute-start.7) | collective-permute-done | bytes 262176 | tf_op jit(solution)/shard_map/ppermute | solution.py:394
  163.1 0.8 maximum_bitcast_fusion
  164.0 3.8 %grad_own.1 = f32[256,4096]{1,0:T(8,128)S(1)} custom-call(s32[6]{0:T(128)S(1)} %stack.45.info_ref.refs_0_, bf16[128,1024]{1,0:T(8,128)(2,1)S(1)} %get-tuple-element.56.refs_0_, bf16[128,1024]{1,0:T(8,128)(2,1)S(1)} %copy-done.13, bf16[128,1024]{1,0:T(8,128)(2,1)S(1)} %copy-done.9, bf16[128,1024]{1,0:T(8,128)(2,1)S(1)} %copy-done.15, ...), custom_call_target="tpu_custom_call" | custom-call | flops 1610612736 | bytes 10485760 | tf_op jit(solution)/shard_map/grad_own/pallas_call | solution.py:369
  167.8 3.6 %fusion = bf16[1,256,4096]{2,1,0:T(8,128)(2,1)} fusion(f32[256,4096]{1,0:T(8,128)S(1)} %grad_own.1, bf16[256,4096]{1,0:T(8,128)(2,1)} %collective-permute-done.24), kind=kLoop, calls=%fused_computation.1 | loop fusion | flops 4194304 | bytes 8388608 | tf_op jit(solution)/shard_map/broadcast_in_dim | solution.py:440
  (69 shorter events, 1.9 us)
Async XLA Ops:
  1.9 25.9 %collective-permute-start.1 = (bf16[128,1024]{1,0:T(8,128)(2,1)S(1)}, bf16[128,1024]{1,0:T(8,128)(2,1)S(1)}, u32[]{:S(2)}, u32[]{:S(2)}) collective-permute-start(bf16[128,1024]{1,0:T(8,128)(2,1)S(1)} %get-tuple-element.74.y1_ref.refs_1_), channel_id=1, source_target_pairs={{0,252},{4,0},{8,4},{12,8},{16,12},{20,16},{24,20},{28,24},{32,28}... | collective-permute-start | bytes 786440 | tf_op jit(solution)/shard_map/ppermute | solution.py:394
  8.2 0.8 copy-start.6
  9.6 7.2 %copy-start.7 = (s32[64,1,128]{2,1,0:T(1,128)S(1)}, s32[64,1,128]{2,1,0:T(1,128)}, u32[]{:S(2)}) copy-start(s32[64,1,128]{2,1,0:T(1,128)} %param.9) | copy-start | bytes 98308
  15.3 12.5 %collective-permute-start = (bf16[128,1024]{1,0:T(8,128)(2,1)S(1)}, bf16[128,1024]{1,0:T(8,128)(2,1)S(1)}, u32[]{:S(2)}, u32[]{:S(2)}) collective-permute-start(bf16[128,1024]{1,0:T(8,128)(2,1)S(1)} %get-tuple-element.35), channel_id=1, source_target_pairs={{0,252},{4,0},{8,4},{12,8},{16,12},{20,16},{24,20},{28,24},{32,28}... | collective-permute-start | bytes 786440 | tf_op jit(solution)/shard_map/ppermute | solution.py:394
  16.8 11.0 %copy-start.20 = (f32[1,1024]{1,0:T(1,128)S(1)}, f32[1,1024]{1,0:T(1,128)}, u32[]{:S(2)}) copy-start(f32[1,1024]{1,0:T(1,128)} %g_ref.5) | copy-start | bytes 12292
  25.7 9.3 %collective-permute-start.9 = (bf16[128,1024]{1,0:T(8,128)(2,1)S(1)}, bf16[128,1024]{1,0:T(8,128)(2,1)S(1)}, u32[]{:S(2)}, u32[]{:S(2)}) collective-permute-start(bf16[128,1024]{1,0:T(8,128)(2,1)S(1)} %get-tuple-element.43), channel_id=1, source_target_pairs={{0,252},{4,0},{8,4},{12,8},{16,12},{20,16},{24,20},{28,24},{32,28}... | collective-permute-start | bytes 786440 | tf_op jit(solution)/shard_map/ppermute | solution.py:394
  25.8 14.8 %collective-permute-start.8 = (bf16[128,1024]{1,0:T(8,128)(2,1)S(1)}, bf16[128,1024]{1,0:T(8,128)(2,1)S(1)}, u32[]{:S(2)}, u32[]{:S(2)}) collective-permute-start(bf16[128,1024]{1,0:T(8,128)(2,1)S(1)} %get-tuple-element.70.refs_3_), channel_id=1, source_target_pairs={{0,252},{4,0},{8,4},{12,8},{16,12},{20,16},{24,20},{28,24},{32,28}... | collective-permute-start | bytes 786440 | tf_op jit(solution)/shard_map/ppermute | solution.py:394
  30.7 20.8 %collective-permute-start.2 = (bf16[128,1024]{1,0:T(8,128)(2,1)S(1)}, bf16[128,1024]{1,0:T(8,128)(2,1)S(1)}, u32[]{:S(2)}, u32[]{:S(2)}) collective-permute-start(bf16[128,1024]{1,0:T(8,128)(2,1)S(1)} %get-tuple-element.37), channel_id=1, source_target_pairs={{0,252},{4,0},{8,4},{12,8},{16,12},{20,16},{24,20},{28,24},{32,28}... | collective-permute-start | bytes 786440 | tf_op jit(solution)/shard_map/ppermute | solution.py:394
  32.6 19.4 %collective-permute-start.3 = (bf16[128,1024]{1,0:T(8,128)(2,1)S(1)}, bf16[128,1024]{1,0:T(8,128)(2,1)S(1)}, u32[]{:S(2)}, u32[]{:S(2)}) collective-permute-start(bf16[128,1024]{1,0:T(8,128)(2,1)S(1)} %collective-permute-done.refs_1_.y1_ref), channel_id=1, source_target_pairs={{0,252},{4,0},{8,4},{12,8},{16,12},{20,16},{24,20},{28,24},{32,28}... | collective-permute-start | bytes 786440 | tf_op jit(solution)/shard_map/ppermute | solution.py:394
  49.4 26.5 %copy-start.8 = (bf16[128,1024]{1,0:T(8,128)(2,1)}, bf16[128,1024]{1,0:T(8,128)(2,1)S(1)}, u32[]{:S(2)}) copy-start(bf16[128,1024]{1,0:T(8,128)(2,1)S(1)} %get-tuple-element.58.refs_2_) | copy-start | bytes 786436
  49.4 9.2 %collective-permute-start.10 = (bf16[128,1024]{1,0:T(8,128)(2,1)S(1)}, bf16[128,1024]{1,0:T(8,128)(2,1)}, u32[]{:S(2)}, u32[]{:S(2)}) collective-permute-start(bf16[128,1024]{1,0:T(8,128)(2,1)S(1)} %get-tuple-element.49), channel_id=1, source_target_pairs={{0,252},{4,0},{8,4},{12,8},{16,12},{20,16},{24,20},{28,24},{32,28}... | collective-permute-start | bytes 786440 | tf_op jit(solution)/shard_map/ppermute | solution.py:394
  49.5 11.8 %collective-permute-start.14 = (bf16[128,1024]{1,0:T(8,128)(2,1)S(1)}, bf16[128,1024]{1,0:T(8,128)(2,1)S(1)}, u32[]{:S(2)}, u32[]{:S(2)}) collective-permute-start(bf16[128,1024]{1,0:T(8,128)(2,1)S(1)} %collective-permute-done.9.c2_ref), channel_id=1, source_target_pairs={{0,252},{4,0},{8,4},{12,8},{16,12},{20,16},{24,20},{28,24},{32,28}... | collective-permute-start | bytes 786440 | tf_op jit(solution)/shard_map/ppermute | solution.py:394
  51.5 24.4 %collective-permute-start.21 = (bf16[128,4096]{1,0:T(8,128)(2,1)S(1)}, bf16[128,4096]{1,0:T(8,128)(2,1)S(1)}, u32[]{:S(2)}, u32[]{:S(2)}) collective-permute-start(bf16[128,4096]{1,0:T(8,128)(2,1)S(1)} %get-tuple-element.62.refs_6_), channel_id=1, source_target_pairs={{0,1},{1,0},{2,3},{3,2},{4,5},{5,4},{6,7},{7,6},{8,9},{9,8},{10,11... | collective-permute-start | bytes 3145736 | tf_op jit(solution)/shard_map/ppermute | solution.py:413
  51.5 9.8 %copy-start.18 = (bf16[128,1024]{1,0:T(8,128)(2,1)}, bf16[128,1024]{1,0:T(8,128)(2,1)S(1)}, u32[]{:S(2)}) copy-start(bf16[128,1024]{1,0:T(8,128)(2,1)S(1)} %collective-permute-done.2.refs_1_.y1_ref) | copy-start | bytes 786436
  51.5 24.4 %collective-permute-start.22 = (bf16[128,4096]{1,0:T(8,128)(2,1)S(1)}, bf16[128,4096]{1,0:T(8,128)(2,1)S(1)}, u32[]{:S(2)}, u32[]{:S(2)}) collective-permute-start(bf16[128,4096]{1,0:T(8,128)(2,1)S(1)} %get-tuple-element.63.refs_8_), channel_id=1, source_target_pairs={{0,1},{1,0},{2,3},{3,2},{4,5},{5,4},{6,7},{7,6},{8,9},{9,8},{10,11... | collective-permute-start | bytes 3145736 | tf_op jit(solution)/shard_map/ppermute | solution.py:413
  71.3 9.7 %copy-start.2 = (bf16[128,4096]{1,0:T(8,128)(2,1)}, bf16[128,4096]{1,0:T(8,128)(2,1)S(1)}, u32[]{:S(2)}) copy-start(bf16[128,4096]{1,0:T(8,128)(2,1)S(1)} %get-tuple-element.64.refs_10_) | copy-start | bytes 3145732
  71.3 9.7 %copy-start.10 = (bf16[128,1024]{1,0:T(8,128)(2,1)}, bf16[128,1024]{1,0:T(8,128)(2,1)S(1)}, u32[]{:S(2)}) copy-start(bf16[128,1024]{1,0:T(8,128)(2,1)S(1)} %get-tuple-element.60.refs_4_) | copy-start | bytes 786436
  71.3 4.6 %collective-permute-start.23 = (bf16[128,4096]{1,0:T(8,128)(2,1)S(1)}, bf16[128,4096]{1,0:T(8,128)(2,1)S(1)}, u32[]{:S(2)}, u32[]{:S(2)}) collective-permute-start(bf16[128,4096]{1,0:T(8,128)(2,1)S(1)} %get-tuple-element.64.refs_10_), channel_id=1, source_target_pairs={{0,1},{1,0},{2,3},{3,2},{4,5},{5,4},{6,7},{7,6},{8,9},{9,8},{10,11... | collective-permute-start | bytes 3145736 | tf_op jit(solution)/shard_map/ppermute | solution.py:413
  71.3 3.0 %collective-permute-start.18 = (bf16[128,1024]{1,0:T(8,128)(2,1)S(1)}, bf16[128,1024]{1,0:T(8,128)(2,1)S(1)}, u32[]{:S(2)}, u32[]{:S(2)}) collective-permute-start(bf16[128,1024]{1,0:T(8,128)(2,1)S(1)} %get-tuple-element.57), channel_id=1, source_target_pairs={{0,1},{1,0},{2,3},{3,2},{4,5},{5,4},{6,7},{7,6},{8,9},{9,8},{10,11... | collective-permute-start | bytes 786440 | tf_op jit(solution)/shard_map/ppermute | solution.py:413
  71.8 2.9 %collective-permute-start.19 = (bf16[128,1024]{1,0:T(8,128)(2,1)S(1)}, bf16[128,1024]{1,0:T(8,128)(2,1)S(1)}, u32[]{:S(2)}, u32[]{:S(2)}) collective-permute-start(bf16[128,1024]{1,0:T(8,128)(2,1)S(1)} %get-tuple-element.59), channel_id=1, source_target_pairs={{0,1},{1,0},{2,3},{3,2},{4,5},{5,4},{6,7},{7,6},{8,9},{9,8},{10,11... | collective-permute-start | bytes 786440 | tf_op jit(solution)/shard_map/ppermute | solution.py:413
  74.4 6.7 %copy-start.12 = (bf16[128,1024]{1,0:T(8,128)(2,1)}, bf16[128,1024]{1,0:T(8,128)(2,1)S(1)}, u32[]{:S(2)}) copy-start(bf16[128,1024]{1,0:T(8,128)(2,1)S(1)} %collective-permute-done.18.refs_1_) | copy-start | bytes 786436
  74.4 1.5 collective-permute-start.20
  74.7 6.3 %copy-start.14 = (bf16[128,1024]{1,0:T(8,128)(2,1)}, bf16[128,1024]{1,0:T(8,128)(2,1)S(1)}, u32[]{:S(2)}) copy-start(bf16[128,1024]{1,0:T(8,128)(2,1)S(1)} %collective-permute-done.19.refs_3_) | copy-start | bytes 786436
  75.9 5.2 %copy-start.16 = (bf16[128,1024]{1,0:T(8,128)(2,1)}, bf16[128,1024]{1,0:T(8,128)(2,1)S(1)}, u32[]{:S(2)}) copy-start(bf16[128,1024]{1,0:T(8,128)(2,1)S(1)} %collective-permute-done.20.refs_5_) | copy-start | bytes 786436
  75.9 5.2 %copy-start = (bf16[128,4096]{1,0:T(8,128)(2,1)}, bf16[128,4096]{1,0:T(8,128)(2,1)S(1)}, u32[]{:S(2)}) copy-start(bf16[128,4096]{1,0:T(8,128)(2,1)S(1)} %collective-permute-done.22.refs_9_) | copy-start | bytes 3145732
  75.9 5.2 %copy-start.4 = (bf16[128,4096]{1,0:T(8,128)(2,1)}, bf16[128,4096]{1,0:T(8,128)(2,1)S(1)}, u32[]{:S(2)}) copy-start(bf16[128,4096]{1,0:T(8,128)(2,1)S(1)} %collective-permute-done.23.refs_11_) | copy-start | bytes 3145732
  81.1 86.7 %collective-permute-start.24 = (bf16[256,4096]{1,0:T(8,128)(2,1)}, bf16[256,4096]{1,0:T(8,128)(2,1)}, u32[]{:S(2)}, u32[]{:S(2)}) collective-permute-start(bf16[256,4096]{1,0:T(8,128)(2,1)} %grad_other.1), channel_id=1, source_target_pairs={{0,2},{1,3},{2,0},{3,1},{4,6},{5,7},{6,4},{7,5},{8,10},{9,11},{10,... | collective-permute-start | bytes 6291464 | tf_op jit(solution)/shard_map/ppermute | solution.py:413
  82.8 4.6 %collective-permute-start.11 = (bf16[128,1024]{1,0:T(8,128)(2,1)}, bf16[128,1024]{1,0:T(8,128)(2,1)}, u32[]{:S(2)}, u32[]{:S(2)}) collective-permute-start(bf16[128,1024]{1,0:T(8,128)(2,1)} %collective-permute-done.10.c2_ref), channel_id=1, source_target_pairs={{0,160},{128,32},{1,161},{129,33},{2,162},{130,34},{3,163},{131,35}} | collective-permute-start | bytes 786440 | tf_op jit(solution)/shard_map/ppermute | solution.py:402
  84.2 55.6 %collective-permute-start.13 = (bf16[128,1024]{1,0:T(8,128)(2,1)}, bf16[128,1024]{1,0:T(8,128)(2,1)}, u32[]{:S(2)}, u32[]{:S(2)}) collective-permute-start(bf16[128,1024]{1,0:T(8,128)(2,1)} %collective-permute-done.10.c2_ref), channel_id=1, source_target_pairs={{4,0},{8,4},{12,8},{16,12},{20,16},{24,20},{28,24},{32,28},{36,32}... | collective-permute-start | bytes 786440 | tf_op jit(solution)/shard_map/ppermute | solution.py:403
  86.1 54.4 %collective-permute-start.15 = (bf16[128,1024]{1,0:T(8,128)(2,1)}, bf16[128,1024]{1,0:T(8,128)(2,1)}, u32[]{:S(2)}, u32[]{:S(2)}) collective-permute-start(bf16[128,1024]{1,0:T(8,128)(2,1)} %get-tuple-element.55), channel_id=1, source_target_pairs={{0,224},{128,96},{1,225},{129,97},{2,226},{130,98},{3,227},{131,99}} | collective-permute-start | bytes 786440 | tf_op jit(solution)/shard_map/ppermute | solution.py:402
  87.4 55.0 %collective-permute-start.12 = (bf16[128,1024]{1,0:T(8,128)(2,1)}, bf16[128,1024]{1,0:T(8,128)(2,1)}, u32[]{:S(2)}, u32[]{:S(2)}) collective-permute-start(bf16[128,1024]{1,0:T(8,128)(2,1)} %collective-permute-done.11), channel_id=1, source_target_pairs={{160,252},{32,124},{161,253},{33,125},{162,254},{34,126},{163,255}... | collective-permute-start | bytes 786440 | tf_op jit(solution)/shard_map/ppermute | solution.py:404
  88.8 1.2 collective-permute-start.25
  90.0 44.9 %collective-permute-start.26 = (f32[1,1024]{1,0:T(1,128)S(1)}, f32[1,1024]{1,0:T(1,128)S(1)}, u32[]{:S(2)}, u32[]{:S(2)}) collective-permute-start(f32[1,1024]{1,0:T(1,128)S(1)} %get-tuple-element.65), channel_id=1, source_target_pairs={{0,2},{1,3},{2,0},{3,1},{4,6},{5,7},{6,4},{7,5},{8,10},{9,11},{10,... | collective-permute-start | bytes 12296 | tf_op jit(solution)/shard_map/ppermute | solution.py:413
  134.9 3.0 %collective-permute-start.27 = (f32[1,1024]{1,0:T(1,128)S(1)}, f32[1,1024]{1,0:T(1,128)S(1)}, u32[]{:S(2)}, u32[]{:S(2)}) collective-permute-start(f32[1,1024]{1,0:T(1,128)S(1)} %get-tuple-element.65), channel_id=1, source_target_pairs={{0,3},{1,2},{2,1},{3,0},{4,7},{5,6},{6,5},{7,4},{8,11},{9,10},{10,... | collective-permute-start | bytes 12296 | tf_op jit(solution)/shard_map/ppermute | solution.py:413
  135.4 28.6 %copy-start.1 = (bf16[128,4096]{1,0:T(8,128)(2,1)S(1)}, bf16[128,4096]{1,0:T(8,128)(2,1)}, u32[]{:S(2)}) copy-start(bf16[128,4096]{1,0:T(8,128)(2,1)} %copy-done) | copy-start | bytes 3145732
  135.4 28.6 %copy-start.3 = (bf16[128,4096]{1,0:T(8,128)(2,1)S(1)}, bf16[128,4096]{1,0:T(8,128)(2,1)}, u32[]{:S(2)}) copy-start(bf16[128,4096]{1,0:T(8,128)(2,1)} %copy-done.2) | copy-start | bytes 3145732
  135.4 28.6 %copy-start.5 = (bf16[128,4096]{1,0:T(8,128)(2,1)S(1)}, bf16[128,4096]{1,0:T(8,128)(2,1)}, u32[]{:S(2)}) copy-start(bf16[128,4096]{1,0:T(8,128)(2,1)} %copy-done.4) | copy-start | bytes 3145732
  135.4 28.6 %copy-start.9 = (bf16[128,1024]{1,0:T(8,128)(2,1)S(1)}, bf16[128,1024]{1,0:T(8,128)(2,1)}, u32[]{:S(2)}) copy-start(bf16[128,1024]{1,0:T(8,128)(2,1)} %copy-done.8) | copy-start | bytes 786436
  135.4 28.6 %copy-start.11 = (bf16[128,1024]{1,0:T(8,128)(2,1)S(1)}, bf16[128,1024]{1,0:T(8,128)(2,1)}, u32[]{:S(2)}) copy-start(bf16[128,1024]{1,0:T(8,128)(2,1)} %copy-done.10) | copy-start | bytes 786436
  135.4 28.6 %copy-start.13 = (bf16[128,1024]{1,0:T(8,128)(2,1)S(1)}, bf16[128,1024]{1,0:T(8,128)(2,1)}, u32[]{:S(2)}) copy-start(bf16[128,1024]{1,0:T(8,128)(2,1)} %copy-done.12) | copy-start | bytes 786436
  135.4 28.6 %copy-start.15 = (bf16[128,1024]{1,0:T(8,128)(2,1)S(1)}, bf16[128,1024]{1,0:T(8,128)(2,1)}, u32[]{:S(2)}) copy-start(bf16[128,1024]{1,0:T(8,128)(2,1)} %copy-done.14) | copy-start | bytes 786436
  135.4 28.6 %copy-start.17 = (bf16[128,1024]{1,0:T(8,128)(2,1)S(1)}, bf16[128,1024]{1,0:T(8,128)(2,1)}, u32[]{:S(2)}) copy-start(bf16[128,1024]{1,0:T(8,128)(2,1)} %copy-done.16) | copy-start | bytes 786436
  137.9 11.3 %collective-permute-start.17 = (bf16[128,1024]{1,0:T(8,128)(2,1)}, bf16[128,1024]{1,0:T(8,128)(2,1)S(1)}, u32[]{:S(2)}, u32[]{:S(2)}) collective-permute-start(bf16[128,1024]{1,0:T(8,128)(2,1)} %get-tuple-element.55), channel_id=1, source_target_pairs={{4,0},{8,4},{12,8},{16,12},{20,16},{24,20},{28,24},{32,28},{36,32}... | collective-permute-start | bytes 786440 | tf_op jit(solution)/shard_map/ppermute | solution.py:403
  139.8 11.5 %collective-permute-start.4 = (bf16[128,1024]{1,0:T(8,128)(2,1)}, bf16[128,1024]{1,0:T(8,128)(2,1)S(1)}, u32[]{:S(2)}, u32[]{:S(2)}) collective-permute-start(bf16[128,1024]{1,0:T(8,128)(2,1)} %copy-done.21), channel_id=1, source_target_pairs={{0,192},{128,64},{1,193},{129,65},{2,194},{130,66},{3,195},{131,67}} | collective-permute-start | bytes 786440 | tf_op jit(solution)/shard_map/ppermute | solution.py:402
  140.5 11.9 %collective-permute-start.16 = (bf16[128,1024]{1,0:T(8,128)(2,1)}, bf16[128,1024]{1,0:T(8,128)(2,1)S(1)}, u32[]{:S(2)}, u32[]{:S(2)}) collective-permute-start(bf16[128,1024]{1,0:T(8,128)(2,1)} %collective-permute-done.15), channel_id=1, source_target_pairs={{224,252},{96,124},{225,253},{97,125},{226,254},{98,126},{227,255}... | collective-permute-start | bytes 786440 | tf_op jit(solution)/shard_map/ppermute | solution.py:404
  142.4 15.6 %collective-permute-start.6 = (bf16[128,1024]{1,0:T(8,128)(2,1)}, bf16[128,1024]{1,0:T(8,128)(2,1)S(1)}, u32[]{:S(2)}, u32[]{:S(2)}) collective-permute-start(bf16[128,1024]{1,0:T(8,128)(2,1)} %copy-done.21), channel_id=1, source_target_pairs={{4,0},{8,4},{12,8},{16,12},{20,16},{24,20},{28,24},{32,28},{36,32}... | collective-permute-start | bytes 786440 | tf_op jit(solution)/shard_map/ppermute | solution.py:403
  149.2 13.9 %collective-permute-start.7 = (bf16[128,1024]{1,0:T(8,128)(2,1)}, bf16[128,1024]{1,0:T(8,128)(2,1)S(1)}, u32[]{:S(2)}, u32[]{:S(2)}) collective-permute-start(bf16[128,1024]{1,0:T(8,128)(2,1)} %copy-done.18), channel_id=1, source_target_pairs={{0,252},{4,0},{8,4},{12,8},{16,12},{20,16},{24,20},{28,24},{32,28}... | collective-permute-start | bytes 786440 | tf_op jit(solution)/shard_map/ppermute | solution.py:394
  151.3 6.7 %collective-permute-start.5 = (bf16[128,1024]{1,0:T(8,128)(2,1)S(1)}, bf16[128,1024]{1,0:T(8,128)(2,1)S(1)}, u32[]{:S(2)}, u32[]{:S(2)}) collective-permute-start(bf16[128,1024]{1,0:T(8,128)(2,1)S(1)} %collective-permute-done.4), channel_id=1, source_target_pairs={{192,252},{64,124},{193,253},{65,125},{194,254},{66,126},{195,255}... | collective-permute-start | bytes 786440 | tf_op jit(solution)/shard_map/ppermute | solution.py:404
  (2 other events, 1.4 us)
where the time goes:
time: 172 us; the launch traced here: 171 us
  waiting for transfers between devices  79.4 us (46%)
  Pallas kernels  48.2 us (28%)
  starting transfers between devices  32.3 us (19%)
  other arithmetic  6.9 us (4%)
  local copies, waits for them, and re-layouts  3.55 us (2%)
    ppermute x10, waiting for transfers between devices, exchange(): return lax.ppermute(value, 'dp', [(r, r ^ bits) for r in range(replicas)])  51.9 us
    pallas_call x3, Pallas kernels, backward(): pl.pallas_call(partial(first_backward_kernel if tick == 0 else backward_k...  27.7 us
    ppermute x9, waiting for transfers between devices, pass_on(): return lax.ppermute(value, 'section', ring)  18.5 us
    ppermute x9, starting transfers between devices, pass_on(): return lax.ppermute(value, 'section', ring)  16 us
    pallas_call x3, Pallas kernels, forward(): pl.pallas_call(partial(first_forward_kernel if first else forward_kernel,...  11.5 us
    pallas_call x2, Pallas kernels, grad_block(): pl.pallas_call(partial(grad_kernel, place), out_shape=shape((QUARTER, 4 *...  8.9 us
    ppermute x3, waiting for transfers between devices, pass_relayed(): near = lax.ppermute(value, 'section', direct)  8.59 us
    ppermute x3, starting transfers between devices, pass_relayed(): near = lax.ppermute(value, 'section', direct)  5.73 us
  transfers between devices with their start and end apart: 28, of which 14 were waited for; matrix products, arithmetic and copies ran while one was open for 2% of the time, Pallas kernels for 25%

commit v1 on v0

--- a/solution.py
+++ b/solution.py
@@ -115,6 +115,14 @@
 
 def forward_kernel(tick, *refs):
     forward_body(RESIDENT, tick, *refs)
+
+
+def last_forward_kernel(tick, *refs):
+    forward_body(RESIDENT, tick, *refs[:2], None, *refs[2:])
+
+
+def last_backward_kernel(tick, *refs):
+    backward_kernel(tick, *refs[:2], None, *refs[2:])
 
 
 def forward_body(copies, tick, info_ref, y1_ref, y2_ref, g_ref, seg_ref, w_ref,
@@ -156,7 +164,10 @@
             copies[chunk].wait()
             out = cols(chunk - 6, CHUNK)
             branch = dot(x2_ref[:, :D], w_ref[:, cols(chunk, CHUNK)])
-            a_ref[:, out] = (y2_ref[:, out].astype(f32) - branch).astype(bf16)
+            if y2_ref is None:
+                a_ref[:, out] = branch
+            else:
+                a_ref[:, out] = (y2_ref[:, out].astype(f32) - branch).astype(bf16)
 
     @pl.when(info_ref[0] == 1)
     def _():
@@ -181,7 +192,10 @@
             for chunk in range(4, 8):
                 copies[chunk].wait()
             add_terms(acc_ref, x2_ref, w_ref, 4, 4)
-        a_ref[...] = (y2_ref[...].astype(f32) - acc_ref[...]).astype(bf16)
+        if y2_ref is None:
+            a_ref[...] = acc_ref[...]
+        else:
+            a_ref[...] = (y2_ref[...].astype(f32) - acc_ref[...]).astype(bf16)
 
 
 def first_backward_kernel(tick, *refs):
@@ -270,7 +284,7 @@
     dg_ref[...] = dg if dg_in_ref is None else dg_in_ref[...] + dg
     scaled = grad_normed * g_ref[...]
     du = inverse * (scaled - unit * jnp.mean(scaled * unit, axis=-1, keepdims=True))
-    c_ref[...] = (c1_ref[...].astype(f32) + du).astype(bf16)
+    c_ref[...] = du if c1_ref is None else (c1_ref[...].astype(f32) + du).astype(bf16)
 
 
 def vmem():
@@ -298,7 +312,9 @@
 
 def forward(tick, info, y1, y2, gain, segments, weight):
     rows = y1.shape[0]
-    first = tick == 0
+    first, last = tick == 0, tick == TICKS - 1
+    ends = [] if last else [held(y2)]
+    kernel = first_forward_kernel if first else last_forward_kernel if last else forward_kernel
     fixed = pltpu.with_memory_space_constraint(weight, pltpu.HBM) if first else None
     saved = (
         pltpu.VMEM((rows, D), bf16), pltpu.VMEM((rows, FF), bf16),
@@ -310,9 +326,9 @@
         resident = (pltpu.VMEM((D, 4 * D), bf16),)
         scratch.append(pltpu.SemaphoreType.DMA((CHUNKS,)))
     return pl.pallas_call(
-        partial(first_forward_kernel if first else forward_kernel, tick),
-        out_shape=(shape((rows, D)),) + saved + resident,
-        in_specs=[smem()] + [vmem()] * 4 + [hbm() if first else vmem()],
+        partial(kernel, tick),
+        out_shape=(shape((rows, D), f32 if last else bf16),) + saved + resident,
+        in_specs=[smem()] + [vmem()] * (3 + len(ends)) + [hbm() if first else vmem()],
         out_specs=(vmem(),) * (5 + len(resident)),
         scratch_shapes=scratch,
         compiler_params=pltpu.CompilerParams(vmem_limit_bytes=16 * MIB),
@@ -320,19 +336,22 @@
             flops=8 * rows * D * D, bytes_accessed=12 * MIB, transcendentals=rows * FF
         ),
         name="tick_forward",
-    )(info, y1, y2, gain, segments, fixed if first else held(weight))
+    )(info, held(y1), *ends, gain, segments, fixed if first else held(weight))
 
 
 def backward(tick, info, y1, c1, c2, gain, segments, dg, saved, weight):
     rows = y1.shape[0]
-    carried = [] if tick == 0 else [dg]
+    first, last = tick == 0, tick == TICKS - 1
+    carried = [] if first else [dg]
+    ends = [] if last else [held(c1)]
+    kernel = first_backward_kernel if first else last_backward_kernel if last else backward_kernel
     return pl.pallas_call(
-        partial(first_backward_kernel if tick == 0 else backward_kernel, tick),
+        partial(kernel, tick),
         out_shape=(
-            shape((rows, D)), shape((rows, 4 * D)), shape((rows, D)),
+            shape((rows, D), f32 if last else bf16), shape((rows, 4 * D)), shape((rows, D)),
             shape((rows, D)), shape((1, D), f32),
         ),
-        in_specs=[smem()] + [vmem()] * (10 + len(carried)),
+        in_specs=[smem()] + [vmem()] * (9 + len(carried) + len(ends)),
         out_specs=(vmem(),) * 5,
         scratch_shapes=[pltpu.VMEM((rows, D), f32)],
         compiler_params=pltpu.CompilerParams(vmem_limit_bytes=16 * MIB),
@@ -340,10 +359,10 @@
             flops=8 * rows * D * D, bytes_accessed=12 * MIB, transcendentals=rows * FF
         ),
         name="tick_backward",
-    )(info, y1, c1, c2, gain, segments, *carried, *saved, held(weight))
-
-
-def grad_kernel(place, info_ref, *refs):
+    )(info, held(y1), *ends, held(c2), gain, segments, *carried, *saved, held(weight))
+
+
+def grad_kernel(place, start, info_ref, *refs):
     count = 2 * TICKS
     lefts, rights, out_ref, turned_ref = refs[:count], refs[count:2 * count], refs[-2], refs[-1]
     rows = lefts[0].shape[0]
@@ -355,29 +374,52 @@
 
     def step(chunk, carry):
         half = jnp.where(chunk >= split, 1, 0)
-        piece = pl.ds(pl.multiple_of(chunk * CHUNK, CHUNK), CHUNK)
-        right = jnp.concatenate([ref[:, piece] for ref in rights], axis=0)
-        out_ref[:, piece] = dot(turned_ref[half], right).astype(out_ref.dtype)
+        right = jnp.concatenate([ref[:, cols(chunk, CHUNK)] for ref in rights], axis=0)
+        out_ref[:, cols(chunk - start, CHUNK)] = dot(turned_ref[half], right).astype(out_ref.dtype)
         return carry
 
-    lax.fori_loop(0, CHUNKS, step, 0)
-
-
-def grad_block(info, lefts, rights, place, dtype):
+    lax.fori_loop(start, start + out_ref.shape[1] // CHUNK, step, 0)
+
+
+def grad_block(info, lefts, rights, place, dtype, start, width):
     rows = lefts[0].shape[0]
     count = len(lefts)
     return pl.pallas_call(
-        partial(grad_kernel, place),
-        out_shape=shape((QUARTER, 4 * D), dtype),
+        partial(grad_kernel, place, start),
+        out_shape=pltpu.VMEM((QUARTER, width * CHUNK), dtype),
         in_specs=[smem()] + [vmem()] * (2 * count),
         out_specs=vmem(),
         scratch_shapes=[pltpu.VMEM((2, QUARTER, count * rows), bf16)],
         compiler_params=pltpu.CompilerParams(vmem_limit_bytes=20 * MIB),
         cost_estimate=pl.CostEstimate(
-            flops=2 * count * rows * D * D, bytes_accessed=10 * MIB, transcendentals=0
+            flops=width * count * rows * D * D // 4, bytes_accessed=width * MIB, transcendentals=0
         ),
         name="grad_own" if place == 0 else "grad_other",
     )(info, *map(held, lefts), *map(held, rights))
+
+
+def finish(own, received, so_far, start, scale):
+    width = received.shape[1] // CHUNK
+
+    def body(own_ref, received_ref, *refs):
+        step = pl.program_id(0)
+        total = own_ref[:, cols(step + start, CHUNK)] + received_ref[:, cols(step, CHUNK)].astype(f32)
+        refs[-1][...] = (total * scale).astype(bf16)
+
+    before = [] if so_far is None else [so_far]
+    return pl.pallas_call(
+        body,
+        out_shape=shape(own.shape),
+        grid=(width,),
+        in_specs=[vmem(), vmem()] + [hbm()] * len(before),
+        out_specs=pl.BlockSpec((QUARTER, CHUNK), lambda j: (0, j + start)),
+        input_output_aliases={2: 0} if before else {},
+        compiler_params=pltpu.CompilerParams(vmem_limit_bytes=16 * MIB),
+        cost_estimate=pl.CostEstimate(
+            flops=width * MIB, bytes_accessed=width * MIB, transcendentals=0
+        ),
+        name="finish",
+    )(held(own), held(received), *before)
 
 
 def shards(streams, cotangents, weights, norm_gains, segment_ids):
@@ -406,7 +448,7 @@
 
     def send(name, value, tick):
         if tick == TICKS - 1 and name in RELAYS:
-            return pass_relayed(value, RELAYS[name] * half // 4)
+            return pass_relayed(value, RELAYS[name] * half // 4 - 1)
         return pass_on(value)
 
     def exchange(value, bits):
@@ -424,20 +466,32 @@
         a, *saved = forward(tick, info, y1, y2, norm_gains, segments, weight)
         if tick == 0:
             weight = saved.pop()
+        if tick == TICKS - 1:
+            a = (y2.astype(f32) - a).astype(bf16)
         next_y1 = send("a", a, tick)
         c, right, keep, give, dg = backward(
             tick, info, y1, c1, c2, norm_gains, segments, dg, saved, weight
         )
+        if tick == TICKS - 1:
+            c = (c1.astype(f32) + c).astype(bf16)
         next_c2 = send("c", c, tick)
         lefts += [keep, exchange(give, 1)]
         rights += [right, exchange(right, 1)]
         y1, y2, c1, c2 = next_y1, next_y2, next_c1, next_c2
     dg_all = dg + exchange(dg, 1) + exchange(dg, 2) + exchange(dg, 3)
-    grad_other = grad_block(info, lefts, rights, 1, bf16)
-    received = exchange(grad_other, 2)
-    grad_own = grad_block(info, lefts, rights, 0, f32)
+    half_width = CHUNKS // 2
+    received = []
+    for part in range(2):
+        grad_other = grad_block(
+            info, lefts, rights, 1, bf16, part * half_width, half_width
+        )
+        received.append(exchange(grad_other, 2))
+    grad_own = grad_block(info, lefts, rights, 0, f32, 0, CHUNKS)
     grad_scale = 1.0 / math.sqrt(TICKS * rows * replicas)
-    weight_grads = ((grad_own + received.astype(f32)) * grad_scale).astype(bf16)[None]
+    weight_grads = None
+    for part in range(2):
+        weight_grads = finish(grad_own, received[part], weight_grads, part * half_width, grad_scale)
+    weight_grads = weight_grads[None]
     gain_grads = lax.dynamic_slice_in_dim(dg_all, replica * QUARTER, QUARTER, 1) * grad_scale
     out_streams = jnp.stack([y1, y2])[:, None, None]
     out_cotangents = jnp.stack([c1, c2])[:, None, None]

time: 172 us -> 178 us (1.035)
  waiting for transfers between devices: 79.4 us -> 59.1 us
  starting transfers between devices: 32.3 us -> 46 us
  local copies, waits for them, and re-layouts: 3.55 us -> 11.9 us
  Pallas kernels: 48.2 us -> 55.2 us
  other arithmetic: 6.9 us -> 4.26 us
    ppermute x10 -> x11, waiting for transfers between devices: 51.9 us -> 28 us  [exchange(): return lax.ppermute(value, 'dp', [(r, r ^ bits) for r in range(replicas)])]
    ppermute x3, starting transfers between devices: 5.73 us -> 21.9 us  [pass_relayed(): near = lax.ppermute(value, 'section', direct)]
    unnamed x44 -> x36, local copies, waits for them, and re-layouts: 2.21 us -> 10.5 us
    pallas_call x8 -> x11, Pallas kernels: 48.2 us -> 55.2 us  [the longest x3 27.9 us: backward(): pl.pallas_call(partial(kernel, tick), out_shape=(shape((rows, D), f32 if...]
    ppermute x9, waiting for transfers between devices: 18.5 us -> 24.2 us  [pass_on(): return lax.ppermute(value, 'section', ring)]
    broadcast_in_dim x1 -> x0, other arithmetic: 3.59 us -> none  [shards(): ((grad_own + received.astype(f32)) * grad_scale).astype(bf16)[None]]
    ppermute x9, starting transfers between devices: 16 us -> 13.7 us  [pass_on(): return lax.ppermute(value, 'section', ring)]
    convert_element_type x0 -> x2, other arithmetic: none -> 1.91 us  [the longest x1 1.16 us: shards(): a = (y2.astype(f32) - a).astype(bf16)]
  transfers between devices with their start and end apart: 28 -> 29, of which waited for: 14 -> 12; matrix products, arithmetic and copies ran while one was open for 2% -> 2% of each run, Pallas kernels for 25% -> 30%
where the time goes in v1:
time: 178 us; the launch traced here: 177 us
  waiting for transfers between devices  59.1 us (33%)
  Pallas kernels  55.2 us (31%)
  starting transfers between devices  46 us (26%)
  local copies, waits for them, and re-layouts  11.9 us (7%)
  other arithmetic  4.26 us (2%)
    ppermute x11, waiting for transfers between devices, exchange(): return lax.ppermute(value, 'dp', [(r, r ^ bits) for r in range(replicas)])  28 us
    pallas_call x3, Pallas kernels, backward(): pl.pallas_call(partial(kernel, tick), out_shape=(shape((rows, D), f32 if...  27.9 us
    ppermute x9, waiting for transfers between devices, pass_on(): return lax.ppermute(value, 'section', ring)  24.2 us
    ppermute x3, starting transfers between devices, pass_relayed(): near = lax.ppermute(value, 'section', direct)  21.9 us
    ppermute x9, starting transfers between devices, pass_on(): return lax.ppermute(value, 'section', ring)  13.7 us
    pallas_call x3, Pallas kernels, grad_block(): pl.pallas_call(partial(grad_kernel, place, start), out_shape=pltpu.VMEM((...  12.4 us
    pallas_call x3, Pallas kernels, forward(): pl.pallas_call(partial(kernel, tick), out_shape=(shape((rows, D), f32 if...  11.7 us
    unnamed x36, local copies, waits for them, and re-layouts  10.5 us
  transfers between devices with their start and end apart: 29, of which 12 were waited for; matrix products, arithmetic and copies ran while one was open for 2% of the time, Pallas kernels for 30%

profile of v1, /device:TPU:6, one launch (start us, length us, event | category | flops | bytes accessed | tf_op | source)
XLA Modules:
  0.0 177.2 jit_solution(4840146779824035818)
XLA Ops:
  0.6 1.3 slice_bitcast_fusion
  1.9 6.2 %collective-permute-start.2 = (bf16[128,1024]{1,0:T(8,128)(2,1)S(1)}, bf16[128,1024]{1,0:T(8,128)(2,1)S(1)}, u32[]{:S(2)}, u32[]{:S(2)}) collective-permute-start(bf16[128,1024]{1,0:T(8,128)(2,1)S(1)} %get-tuple-element.74.y1_ref.refs_1_), channel_id=1, source_target_pairs={{0,252},{4,0},{8,4},{12,8},{16,12},{20,16},{24,20},{28,24},{32,28}... | collective-permute-start | bytes 786440 | tf_op jit(solution)/shard_map/ppermute | solution.py:436
  8.2 0.8 copy-done.10
  9.6 5.7 %tick_forward.3 = (bf16[128,1024]{1,0:T(8,128)(2,1)S(1)}, bf16[128,1024]{1,0:T(8,128)(2,1)S(1)}, bf16[128,2048]{1,0:T(8,128)(2,1)S(1)}, f32[128,2048]{1,0:T(8,12...) custom-call(s32[6]{0:T(128)S(1)} %stack.45.info_ref.refs_0_, ...), custom_call_target="tpu_custom_call" | custom-call | flops 1073741824 | bytes 12582912 | tf_op jit(solution)/shard_map/tick_forward/pallas_call | solution.py:328
  15.3 1.5 collective-permute-start
  16.8 8.9 %tick_backward.3 = (bf16[128,1024]{1,0:T(8,128)(2,1)S(1)}, bf16[128,4096]{1,0:T(8,128)(2,1)S(1)}, bf16[128,1024]{1,0:T(8,128)(2,1)S(1)}, bf16[128,1024]{1,0:T(8,128)(2,1)S(1)}, f32[1,1024]{1,0:T(1,128)S(1)}) custom-call(s32[6]{0:T(128)S(1)} %stack.45.info_ref.refs_0_, bf16[128,1024]{1,0:T(8,128)(2,1)S(1)} %get-tuple-element.74.y1_ref.refs_1_, ...), custom_call_target="tpu_custom_call" | custom-call | flops 1073741824 | bytes 12582912 | tf_op jit(solution)/shard_map/tick_backward/pallas_call | solution.py:348
  25.8 2.0 %collective-permute-start.8 = (bf16[128,1024]{1,0:T(8,128)(2,1)S(1)}, bf16[128,1024]{1,0:T(8,128)(2,1)S(1)}, u32[]{:S(2)}, u32[]{:S(2)}) collective-permute-start(bf16[128,1024]{1,0:T(8,128)(2,1)S(1)} %get-tuple-element.71.refs_3_), channel_id=1, source_target_pairs={{0,252},{4,0},{8,4},{12,8},{16,12},{20,16},{24,20},{28,24},{32,28}... | collective-permute-start | bytes 786440 | tf_op jit(solution)/shard_map/ppermute | solution.py:436
  27.8 3.0 %tick_forward.4 = (bf16[128,1024]{1,0:T(8,128)(2,1)S(1)}, bf16[128,1024]{1,0:T(8,128)(2,1)S(1)}, bf16[128,2048]{1,0:T(8,128)(2,1)S(1)}, f32[128,2048]{1,0:T(8,128)S(1)}, bf16[128,3072]{1,0:T(8,128)(2,1)S(1)}) custom-call(s32[6]{0:T(128)S(1)} %stack.45.info_ref.refs_0_, bf16[128,1024]{1,0:T(8,128)(2,1)S(1)} %collective-permute-done.refs_1_.y1_ref, ...), custom_call_target="tpu_custom_call" | custom-call | flops 1073741824 | bytes 12582912 | tf_op jit(solution)/shard_map/tick_forward/pallas_call | solution.py:328
  30.8 1.9 %collective-permute-start.3 = (bf16[128,1024]{1,0:T(8,128)(2,1)S(1)}, bf16[128,1024]{1,0:T(8,128)(2,1)S(1)}, u32[]{:S(2)}, u32[]{:S(2)}) collective-permute-start(bf16[128,1024]{1,0:T(8,128)(2,1)S(1)} %get-tuple-element.37), channel_id=1, source_target_pairs={{0,252},{4,0},{8,4},{12,8},{16,12},{20,16},{24,20},{28,24},{32,28}... | collective-permute-start | bytes 786440 | tf_op jit(solution)/shard_map/ppermute | solution.py:436
  32.6 2.3 %collective-permute-done.9.c2_ref = bf16[128,1024]{1,0:T(8,128)(2,1)S(1)} collective-permute-done((bf16[128,1024]{1,0:T(8,128)(2,1)S(1)}, bf16[128,1024]{1,0:T(8,128)(2,1)S(1)}, u32[]{:S(2)}, u32[]{:S(2)}) %collective-permute-start.9) | collective-permute-done | bytes 262176 | tf_op jit(solution)/shard_map/ppermute | solution.py:436
  34.9 5.6 %collective-permute-done.8.c1_ref = bf16[128,1024]{1,0:T(8,128)(2,1)S(1)} collective-permute-done((bf16[128,1024]{1,0:T(8,128)(2,1)S(1)}, bf16[128,1024]{1,0:T(8,128)(2,1)S(1)}, u32[]{:S(2)}, u32[]{:S(2)}) %collective-permute-start.8) | collective-permute-done | bytes 262176 | tf_op jit(solution)/shard_map/ppermute | solution.py:436
  40.5 8.9 %tick_backward.4 = (bf16[128,1024]{1,0:T(8,128)(2,1)S(1)}, bf16[128,4096]{1,0:T(8,128)(2,1)S(1)}, bf16[128,1024]{1,0:T(8,128)(2,1)S(1)}, bf16[128,1024]{1,0:T(8,128)(2,1)S(1)}, f32[1,1024]{1,0:T(1,128)S(1)}) custom-call(s32[6]{0:T(128)S(1)} %stack.45.info_ref.refs_0_, bf16[128,1024]{1,0:T(8,128)(2,1)S(1)} %collective-permute-done.refs_1_.y1_ref, ...), custom_call_target="tpu_custom_call" | custom-call | flops 1073741824 | bytes 12582912 | tf_op jit(solution)/shard_map/tick_backward/pallas_call | solution.py:348
  51.1 3.0 %tick_forward.5 = (f32[128,1024]{1,0:T(8,128)S(1)}, bf16[128,1024]{1,0:T(8,128)(2,1)S(1)}, bf16[128,2048]{1,0:T(8,128)(2,1)S(1)}, f32[128,2048]{1,0:T(8,128)S(1)}, bf16[128,3072]{1,0:T(8,128)(2,1)S(1)}) custom-call(s32[6]{0:T(128)S(1)} %stack.45.info_ref.refs_0_, bf16[128,1024]{1,0:T(8,128)(2,1)S(1)} %collective-permute-done.3.refs_1_, ...), custom_call_target="tpu_custom_call" | custom-call | flops 1073741824 | bytes 12582912 | tf_op jit(solution)/shard_map/tick_forward/pallas_call | solution.py:328
  54.2 0.8 copy-done.14
  55.0 1.6 collective-permute-done.10.refs_2_
  56.6 10.1 %tick_backward.5 = (f32[128,1024]{1,0:T(8,128)S(1)}, bf16[128,4096]{1,0:T(8,128)(2,1)}, bf16[128,1024]{1,0:T(8,128)(2,1)S(1)}, bf16[128,1024]{1,0:T(8,128)(2,1)S(1)}, f32[1,1024]{1,0:T(1,128)S(1)}) custom-call(s32[6]{0:T(128)S(1)} %stack.45.info_ref.refs_0_, bf16[128,1024]{1,0:T(8,128)(2,1)S(1)} %collective-permute-done.3.refs_1_, ...), custom_call_target="tpu_custom_call" | custom-call | flops 1073741824 | bytes 12582912 | tf_op jit(solution)/shard_map/tick_backward/pallas_call | solution.py:348
  67.4 0.7 copy-done.2
  68.9 2.0 %collective-permute-start.1 = (bf16[128,1024]{1,0:T(8,128)(2,1)S(1)}, bf16[128,1024]{1,0:T(8,128)(2,1)S(1)}, u32[]{:S(2)}, u32[]{:S(2)}) collective-permute-start(bf16[128,1024]{1,0:T(8,128)(2,1)S(1)} %collective-permute-done.refs_1_.y1_ref), channel_id=1, source_target_pairs={{0,252},{4,0},{8,4},{12,8},{16,12},{20,16},{24,20},{28,24},{32,28}... | collective-permute-start | bytes 786440 | tf_op jit(solution)/shard_map/ppermute | solution.py:436
  70.9 6.4 %collective-permute-done.14 = bf16[128,1024]{1,0:T(8,128)(2,1)S(1)} collective-permute-done((bf16[128,1024]{1,0:T(8,128)(2,1)S(1)}, bf16[128,1024]{1,0:T(8,128)(2,1)S(1)}, u32[]{:S(2)}, u32[]{:S(2)}) %collective-permute-start.14) | collective-permute-done | bytes 262176 | tf_op jit(solution)/shard_map/ppermute | solution.py:436
  77.3 5.2 %collective-permute-done.1 = bf16[128,1024]{1,0:T(8,128)(2,1)S(1)} collective-permute-done((bf16[128,1024]{1,0:T(8,128)(2,1)S(1)}, bf16[128,1024]{1,0:T(8,128)(2,1)S(1)}, u32[]{:S(2)}, u32[]{:S(2)}) %collective-permute-start.1) | collective-permute-done | bytes 262176 | tf_op jit(solution)/shard_map/ppermute | solution.py:436
  82.5 1.2 collective-permute-done.26
  83.7 1.6 collective-permute-start.27
  85.2 2.0 %collective-permute-done.27 = f32[1,1024]{1,0:T(1,128)S(1)} collective-permute-done((f32[1,1024]{1,0:T(1,128)S(1)}, f32[1,1024]{1,0:T(1,128)S(1)}, u32[]{:S(2)}, u32[]{:S(2)}) %collective-permute-start.27) | collective-permute-done | bytes 4128 | tf_op jit(solution)/shard_map/ppermute | solution.py:455
  87.5 0.8 add_convert_fusion
  88.2 2.1 %collective-permute-done.28 = f32[1,1024]{1,0:T(1,128)S(1)} collective-permute-done((f32[1,1024]{1,0:T(1,128)S(1)}, f32[1,1024]{1,0:T(1,128)S(1)}, u32[]{:S(2)}, u32[]{:S(2)}) %collective-permute-start.28) | collective-permute-done | bytes 4128 | tf_op jit(solution)/shard_map/ppermute | solution.py:455
  90.3 1.4 collective-permute-start.11
  92.4 1.4 collective-permute-start.15
  93.7 1.2 subtract_convert_fusion
  94.9 4.3 %collective-permute-start.13 = (bf16[128,1024]{1,0:T(8,128)(2,1)}, bf16[128,1024]{1,0:T(8,128)(2,1)S(1)}, u32[]{:S(2)}, u32[]{:S(2)}) collective-permute-start(bf16[128,1024]{1,0:T(8,128)(2,1)} %collective-permute-done.10.refs_2_), channel_id=1, source_target_pairs={{4,0},{8,4},{12,8},{16,12},{20,16},{24,20},{28,24},{32,28},{36,32}... | collective-permute-start | bytes 786440 | tf_op jit(solution)/shard_map/ppermute | solution.py:445
  100.4 15.1 %collective-permute-start.17 = (bf16[128,1024]{1,0:T(8,128)(2,1)}, bf16[128,1024]{1,0:T(8,128)(2,1)S(1)}, u32[]{:S(2)}, u32[]{:S(2)}) collective-permute-start(bf16[128,1024]{1,0:T(8,128)(2,1)} %add_convert_fusion), channel_id=1, source_target_pairs={{4,0},{8,4},{12,8},{16,12},{20,16},{24,20},{28,24},{32,28},{36,32}... | collective-permute-start | bytes 786440 | tf_op jit(solution)/shard_map/ppermute | solution.py:445
  116.9 0.9 copy-done.1
  117.9 0.9 copy-done.3
  118.8 0.9 copy-done.5
  119.8 0.9 copy-done.7
  120.7 0.9 copy-done.9
  121.7 3.6 %grad_other.3 = bf16[256,2048]{1,0:T(8,128)(2,1)S(1)} custom-call(s32[6]{0:T(128)S(1)} %stack.45.info_ref.refs_0_, bf16[128,1024]{1,0:T(8,128)(2,1)S(1)} %get-tuple-element.56.refs_0_, bf16[128,1024]{1,0:T(8,128)(2,1)S(1)} %copy-done.3, bf16[128,1024]{1,0:T(8,128)(2,1)S(1)} %copy-done.1, bf16[128,1024]{1,0:T(8,128)(2,1)S(1)} %copy-done.5, ...), custom_call_target="tpu_custom_call" | custom-call | flops 805306368 | bytes 4194304 | tf_op jit(solution)/shard_map/grad_other/pallas_call | solution.py:387
  125.3 3.7 %grad_other.2 = bf16[256,2048]{1,0:T(8,128)(2,1)S(1)} custom-call(s32[6]{0:T(128)S(1)} %stack.45.info_ref.refs_0_, bf16[128,1024]{1,0:T(8,128)(2,1)S(1)} %get-tuple-element.56.refs_0_, bf16[128,1024]{1,0:T(8,128)(2,1)S(1)} %copy-done.3, bf16[128,1024]{1,0:T(8,128)(2,1)S(1)} %copy-done.1, bf16[128,1024]{1,0:T(8,128)(2,1)S(1)} %copy-done.5, ...), custom_call_target="tpu_custom_call" | custom-call | flops 805306368 | bytes 4194304 | tf_op jit(solution)/shard_map/grad_other/pallas_call | solution.py:387
  129.6 1.5 collective-permute-start.24
  131.2 2.5 %collective-permute-start.6 = (bf16[128,1024]{1,0:T(8,128)(2,1)S(1)}, bf16[128,1024]{1,0:T(8,128)(2,1)S(1)}, u32[]{:S(2)}, u32[]{:S(2)}) collective-permute-start(bf16[128,1024]{1,0:T(8,128)(2,1)S(1)} %subtract_convert_fusion), channel_id=1, source_target_pairs={{4,0},{8,4},{12,8},{16,12},{20,16},{24,20},{28,24},{32,28},{36,32}... | collective-permute-start | bytes 786440 | tf_op jit(solution)/shard_map/ppermute | solution.py:445
  134.6 0.8 maximum_bitcast_fusion.1
  135.4 6.8 %collective-permute-done.6 = bf16[128,1024]{1,0:T(8,128)(2,1)S(1)} collective-permute-done((bf16[128,1024]{1,0:T(8,128)(2,1)S(1)}, bf16[128,1024]{1,0:T(8,128)(2,1)S(1)}, u32[]{:S(2)}, u32[]{:S(2)}) %collective-permute-start.6) | collective-permute-done | bytes 262176 | tf_op jit(solution)/shard_map/ppermute | solution.py:445
  142.3 3.0 %collective-permute-done.7 = bf16[128,1024]{1,0:T(8,128)(2,1)S(1)} collective-permute-done((bf16[128,1024]{1,0:T(8,128)(2,1)S(1)}, bf16[128,1024]{1,0:T(8,128)(2,1)S(1)}, u32[]{:S(2)}, u32[]{:S(2)}) %collective-permute-start.7) | collective-permute-done | bytes 262176 | tf_op jit(solution)/shard_map/ppermute | solution.py:436
  145.3 0.8 maximum_bitcast_fusion
  146.1 5.1 %grad_own.1.own_ref = f32[256,4096]{1,0:T(8,128)S(1)} custom-call(s32[6]{0:T(128)S(1)} %stack.45.info_ref.refs_0_, bf16[128,1024]{1,0:T(8,128)(2,1)S(1)} %get-tuple-element.56.refs_0_, bf16[128,1024]{1,0:T(8,128)(2,1)S(1)} %copy-done.3, bf16[128,1024]{1,0:T(8,128)(2,1)S(1)} %copy-done.1, bf16[128,1024]{1,0:T(8,128)(2,1)S(1)} %copy-done.5, ...), custom_call_target="tpu_custom_call" | custom-call | flops 1610612736 | bytes 8388608 | tf_op jit(solution)/shard_map/grad_own/pallas_call | solution.py:387
  151.2 3.9 %collective-permute-done.25.received_ref = bf16[256,2048]{1,0:T(8,128)(2,1)S(1)} collective-permute-done((bf16[256,2048]{1,0:T(8,128)(2,1)S(1)}, bf16[256,2048]{1,0:T(8,128)(2,1)S(1)}, u32[]{:S(2)}, u32[]{:S(2)}) %collective-permute-start.25) | collective-permute-done | bytes 1048608 | tf_op jit(solution)/shard_map/ppermute | solution.py:455
  155.1 1.6 finish.2.refs_0_
  156.7 18.9 %collective-permute-done.24.received_ref = bf16[256,2048]{1,0:T(8,128)(2,1)S(1)} collective-permute-done((bf16[256,2048]{1,0:T(8,128)(2,1)S(1)}, bf16[256,2048]{1,0:T(8,128)(2,1)S(1)}, u32[]{:S(2)}, u32[]{:S(2)}) %collective-permute-start.24) | collective-permute-done | bytes 1048608 | tf_op jit(solution)/shard_map/ppermute | solution.py:455
  175.6 1.6 finish.3
  (67 shorter events, 9.0 us)
Async XLA Ops:
  1.9 25.9 %collective-permute-start.2 = (bf16[128,1024]{1,0:T(8,128)(2,1)S(1)}, bf16[128,1024]{1,0:T(8,128)(2,1)S(1)}, u32[]{:S(2)}, u32[]{:S(2)}) collective-permute-start(bf16[128,1024]{1,0:T(8,128)(2,1)S(1)} %get-tuple-element.74.y1_ref.refs_1_), channel_id=1, source_target_pairs={{0,252},{4,0},{8,4},{12,8},{16,12},{20,16},{24,20},{28,24},{32,28}... | collective-permute-start | bytes 786440 | tf_op jit(solution)/shard_map/ppermute | solution.py:436
  8.2 0.8 copy-start.10
  8.9 0.7 copy-start.15
  9.6 7.2 %copy-start.11 = (s32[64,1,128]{2,1,0:T(1,128)S(1)}, s32[64,1,128]{2,1,0:T(1,128)}, u32[]{:S(2)}) copy-start(s32[64,1,128]{2,1,0:T(1,128)} %param.9) | copy-start | bytes 98308
  9.6 7.2 %copy-start.16 = (f32[1,1024]{1,0:T(1,128)S(1)}, f32[1,1024]{1,0:T(1,128)}, u32[]{:S(2)}) copy-start(f32[1,1024]{1,0:T(1,128)} %refs_3_.3) | copy-start | bytes 12292
  15.3 12.4 %collective-permute-start = (bf16[128,1024]{1,0:T(8,128)(2,1)S(1)}, bf16[128,1024]{1,0:T(8,128)(2,1)S(1)}, u32[]{:S(2)}, u32[]{:S(2)}) collective-permute-start(bf16[128,1024]{1,0:T(8,128)(2,1)S(1)} %get-tuple-element.35), channel_id=1, source_target_pairs={{0,252},{4,0},{8,4},{12,8},{16,12},{20,16},{24,20},{28,24},{32,28}... | collective-permute-start | bytes 786440 | tf_op jit(solution)/shard_map/ppermute | solution.py:436
  25.7 9.3 %collective-permute-start.9 = (bf16[128,1024]{1,0:T(8,128)(2,1)S(1)}, bf16[128,1024]{1,0:T(8,128)(2,1)S(1)}, u32[]{:S(2)}, u32[]{:S(2)}) collective-permute-start(bf16[128,1024]{1,0:T(8,128)(2,1)S(1)} %get-tuple-element.43), channel_id=1, source_target_pairs={{0,252},{4,0},{8,4},{12,8},{16,12},{20,16},{24,20},{28,24},{32,28}... | collective-permute-start | bytes 786440 | tf_op jit(solution)/shard_map/ppermute | solution.py:436
  25.8 14.8 %collective-permute-start.8 = (bf16[128,1024]{1,0:T(8,128)(2,1)S(1)}, bf16[128,1024]{1,0:T(8,128)(2,1)S(1)}, u32[]{:S(2)}, u32[]{:S(2)}) collective-permute-start(bf16[128,1024]{1,0:T(8,128)(2,1)S(1)} %get-tuple-element.71.refs_3_), channel_id=1, source_target_pairs={{0,252},{4,0},{8,4},{12,8},{16,12},{20,16},{24,20},{28,24},{32,28}... | collective-permute-start | bytes 786440 | tf_op jit(solution)/shard_map/ppermute | solution.py:436
  30.8 19.9 %collective-permute-start.3 = (bf16[128,1024]{1,0:T(8,128)(2,1)S(1)}, bf16[128,1024]{1,0:T(8,128)(2,1)S(1)}, u32[]{:S(2)}, u32[]{:S(2)}) collective-permute-start(bf16[128,1024]{1,0:T(8,128)(2,1)S(1)} %get-tuple-element.37), channel_id=1, source_target_pairs={{0,252},{4,0},{8,4},{12,8},{16,12},{20,16},{24,20},{28,24},{32,28}... | collective-permute-start | bytes 786440 | tf_op jit(solution)/shard_map/ppermute | solution.py:436
  49.4 0.7 copy-start
  50.1 6.5 %collective-permute-start.10 = (bf16[128,1024]{1,0:T(8,128)(2,1)S(1)}, bf16[128,1024]{1,0:T(8,128)(2,1)}, u32[]{:S(2)}, u32[]{:S(2)}) collective-permute-start(bf16[128,1024]{1,0:T(8,128)(2,1)S(1)} %get-tuple-element.49), channel_id=1, source_target_pairs={{0,252},{4,0},{8,4},{12,8},{16,12},{20,16},{24,20},{28,24},{32,28}... | collective-permute-start | bytes 786440 | tf_op jit(solution)/shard_map/ppermute | solution.py:436
  50.1 50.3 %collective-permute-start.21 = (bf16[128,4096]{1,0:T(8,128)(2,1)S(1)}, bf16[128,4096]{1,0:T(8,128)(2,1)S(1)}, u32[]{:S(2)}, u32[]{:S(2)}) collective-permute-start(bf16[128,4096]{1,0:T(8,128)(2,1)S(1)} %get-tuple-element.62.refs_6_), channel_id=1, source_target_pairs={{0,1},{1,0},{2,3},{3,2},{4,5},{5,4},{6,7},{7,6},{8,9},{9,8},{10,11... | collective-permute-start | bytes 3145736 | tf_op jit(solution)/shard_map/ppermute | solution.py:455
  50.1 17.3 %collective-permute-start.18 = (bf16[128,1024]{1,0:T(8,128)(2,1)S(1)}, bf16[128,1024]{1,0:T(8,128)(2,1)S(1)}, u32[]{:S(2)}, u32[]{:S(2)}) collective-permute-start(bf16[128,1024]{1,0:T(8,128)(2,1)S(1)} %get-tuple-element.57), channel_id=1, source_target_pairs={{0,1},{1,0},{2,3},{3,2},{4,5},{5,4},{6,7},{7,6},{8,9},{9,8},{10,11... | collective-permute-start | bytes 786440 | tf_op jit(solution)/shard_map/ppermute | solution.py:455
  50.6 64.9 %collective-permute-start.22 = (bf16[128,4096]{1,0:T(8,128)(2,1)S(1)}, bf16[128,4096]{1,0:T(8,128)(2,1)}, u32[]{:S(2)}, u32[]{:S(2)}) collective-permute-start(bf16[128,4096]{1,0:T(8,128)(2,1)S(1)} %get-tuple-element.63.refs_8_), channel_id=1, source_target_pairs={{0,1},{1,0},{2,3},{3,2},{4,5},{5,4},{6,7},{7,6},{8,9},{9,8},{10,11... | collective-permute-start | bytes 3145736 | tf_op jit(solution)/shard_map/ppermute | solution.py:455
  50.6 6.0 %copy-start.12 = (bf16[128,1024]{1,0:T(8,128)(2,1)}, bf16[128,1024]{1,0:T(8,128)(2,1)S(1)}, u32[]{:S(2)}) copy-start(bf16[128,1024]{1,0:T(8,128)(2,1)S(1)} %collective-permute-done.3.refs_1_) | copy-start | bytes 786436
  50.6 17.5 %collective-permute-start.19 = (bf16[128,1024]{1,0:T(8,128)(2,1)S(1)}, bf16[128,1024]{1,0:T(8,128)(2,1)S(1)}, u32[]{:S(2)}, u32[]{:S(2)}) collective-permute-start(bf16[128,1024]{1,0:T(8,128)(2,1)S(1)} %get-tuple-element.59), channel_id=1, source_target_pairs={{0,1},{1,0},{2,3},{3,2},{4,5},{5,4},{6,7},{7,6},{8,9},{9,8},{10,11... | collective-permute-start | bytes 786440 | tf_op jit(solution)/shard_map/ppermute | solution.py:455
  54.2 0.8 copy-start.14
  66.7 0.7 copy-start.6
  67.4 48.8 %collective-permute-start.23 = (bf16[128,4096]{1,0:T(8,128)(2,1)}, bf16[128,4096]{1,0:T(8,128)(2,1)}, u32[]{:S(2)}, u32[]{:S(2)}) collective-permute-start(bf16[128,4096]{1,0:T(8,128)(2,1)} %get-tuple-element.64.refs_10_), channel_id=1, source_target_pairs={{0,1},{1,0},{2,3},{3,2},{4,5},{5,4},{6,7},{7,6},{8,9},{9,8},{10,11... | collective-permute-start | bytes 3145736 | tf_op jit(solution)/shard_map/ppermute | solution.py:455
  67.4 0.7 copy-start.2
  68.1 9.2 %collective-permute-start.14 = (bf16[128,1024]{1,0:T(8,128)(2,1)S(1)}, bf16[128,1024]{1,0:T(8,128)(2,1)S(1)}, u32[]{:S(2)}, u32[]{:S(2)}) collective-permute-start(bf16[128,1024]{1,0:T(8,128)(2,1)S(1)} %collective-permute-done.9.c2_ref), channel_id=1, source_target_pairs={{0,252},{4,0},{8,4},{12,8},{16,12},{20,16},{24,20},{28,24},{32,28}... | collective-permute-start | bytes 786440 | tf_op jit(solution)/shard_map/ppermute | solution.py:436
  68.2 0.7 copy-start.4
  68.9 13.6 %collective-permute-start.1 = (bf16[128,1024]{1,0:T(8,128)(2,1)S(1)}, bf16[128,1024]{1,0:T(8,128)(2,1)S(1)}, u32[]{:S(2)}, u32[]{:S(2)}) collective-permute-start(bf16[128,1024]{1,0:T(8,128)(2,1)S(1)} %collective-permute-done.refs_1_.y1_ref), channel_id=1, source_target_pairs={{0,252},{4,0},{8,4},{12,8},{16,12},{20,16},{24,20},{28,24},{32,28}... | collective-permute-start | bytes 786440 | tf_op jit(solution)/shard_map/ppermute | solution.py:436
  77.3 14.3 %collective-permute-start.20 = (bf16[128,1024]{1,0:T(8,128)(2,1)S(1)}, bf16[128,1024]{1,0:T(8,128)(2,1)S(1)}, u32[]{:S(2)}, u32[]{:S(2)}) collective-permute-start(bf16[128,1024]{1,0:T(8,128)(2,1)S(1)} %get-tuple-element.61), channel_id=1, source_target_pairs={{0,1},{1,0},{2,3},{3,2},{4,5},{5,4},{6,7},{7,6},{8,9},{9,8},{10,11... | collective-permute-start | bytes 786440 | tf_op jit(solution)/shard_map/ppermute | solution.py:455
  82.5 9.2 %copy-start.17 = (bf16[128,1024]{1,0:T(8,128)(2,1)}, bf16[128,1024]{1,0:T(8,128)(2,1)S(1)}, u32[]{:S(2)}) copy-start(bf16[128,1024]{1,0:T(8,128)(2,1)S(1)} %collective-permute-done.1) | copy-start | bytes 786436
  82.5 1.2 collective-permute-start.26
  83.7 3.6 %collective-permute-start.27 = (f32[1,1024]{1,0:T(1,128)S(1)}, f32[1,1024]{1,0:T(1,128)S(1)}, u32[]{:S(2)}, u32[]{:S(2)}) collective-permute-start(f32[1,1024]{1,0:T(1,128)S(1)} %get-tuple-element.65), channel_id=1, source_target_pairs={{0,2},{1,3},{2,0},{3,1},{4,6},{5,7},{6,4},{7,5},{8,10},{9,11},{10,... | collective-permute-start | bytes 12296 | tf_op jit(solution)/shard_map/ppermute | solution.py:455
  87.3 3.0 %collective-permute-start.28 = (f32[1,1024]{1,0:T(1,128)S(1)}, f32[1,1024]{1,0:T(1,128)S(1)}, u32[]{:S(2)}, u32[]{:S(2)}) collective-permute-start(f32[1,1024]{1,0:T(1,128)S(1)} %get-tuple-element.65), channel_id=1, source_target_pairs={{0,3},{1,2},{2,1},{3,0},{4,7},{5,6},{6,5},{7,4},{8,11},{9,10},{10,... | collective-permute-start | bytes 12296 | tf_op jit(solution)/shard_map/ppermute | solution.py:455
  90.3 4.6 %collective-permute-start.11 = (bf16[128,1024]{1,0:T(8,128)(2,1)}, bf16[128,1024]{1,0:T(8,128)(2,1)}, u32[]{:S(2)}, u32[]{:S(2)}) collective-permute-start(bf16[128,1024]{1,0:T(8,128)(2,1)} %collective-permute-done.10.refs_2_), channel_id=1, source_target_pairs={{0,156},{128,28},{1,157},{129,29},{2,158},{130,30},{3,159},{131,31}} | collective-permute-start | bytes 786440 | tf_op jit(solution)/shard_map/ppermute | solution.py:444
  91.7 0.7 copy-start.8
  92.4 6.8 %collective-permute-start.15 = (bf16[128,1024]{1,0:T(8,128)(2,1)}, bf16[128,1024]{1,0:T(8,128)(2,1)}, u32[]{:S(2)}, u32[]{:S(2)}) collective-permute-start(bf16[128,1024]{1,0:T(8,128)(2,1)} %add_convert_fusion), channel_id=1, source_target_pairs={{0,220},{128,92},{1,221},{129,93},{2,222},{130,94},{3,223},{131,95}} | collective-permute-start | bytes 786440 | tf_op jit(solution)/shard_map/ppermute | solution.py:444
  94.9 34.1 %collective-permute-start.13 = (bf16[128,1024]{1,0:T(8,128)(2,1)}, bf16[128,1024]{1,0:T(8,128)(2,1)S(1)}, u32[]{:S(2)}, u32[]{:S(2)}) collective-permute-start(bf16[128,1024]{1,0:T(8,128)(2,1)} %collective-permute-done.10.refs_2_), channel_id=1, source_target_pairs={{4,0},{8,4},{12,8},{16,12},{20,16},{24,20},{28,24},{32,28},{36,32}... | collective-permute-start | bytes 786440 | tf_op jit(solution)/shard_map/ppermute | solution.py:445
  99.2 30.4 %collective-permute-start.12 = (bf16[128,1024]{1,0:T(8,128)(2,1)}, bf16[128,1024]{1,0:T(8,128)(2,1)S(1)}, u32[]{:S(2)}, u32[]{:S(2)}) collective-permute-start(bf16[128,1024]{1,0:T(8,128)(2,1)} %collective-permute-done.11), channel_id=1, source_target_pairs={{156,252},{28,124},{157,253},{29,125},{158,254},{30,126},{159,255}... | collective-permute-start | bytes 786440 | tf_op jit(solution)/shard_map/ppermute | solution.py:446
  100.4 30.7 %collective-permute-start.17 = (bf16[128,1024]{1,0:T(8,128)(2,1)}, bf16[128,1024]{1,0:T(8,128)(2,1)S(1)}, u32[]{:S(2)}, u32[]{:S(2)}) collective-permute-start(bf16[128,1024]{1,0:T(8,128)(2,1)} %add_convert_fusion), channel_id=1, source_target_pairs={{4,0},{8,4},{12,8},{16,12},{20,16},{24,20},{28,24},{32,28},{36,32}... | collective-permute-start | bytes 786440 | tf_op jit(solution)/shard_map/ppermute | solution.py:445
  115.6 18.2 %collective-permute-start.4 = (bf16[128,1024]{1,0:T(8,128)(2,1)S(1)}, bf16[128,1024]{1,0:T(8,128)(2,1)S(1)}, u32[]{:S(2)}, u32[]{:S(2)}) collective-permute-start(bf16[128,1024]{1,0:T(8,128)(2,1)S(1)} %subtract_convert_fusion), channel_id=1, source_target_pairs={{0,188},{128,60},{1,189},{129,61},{2,190},{130,62},{3,191},{131,63}} | collective-permute-start | bytes 786440 | tf_op jit(solution)/shard_map/ppermute | solution.py:444
  116.2 17.6 %collective-permute-start.16 = (bf16[128,1024]{1,0:T(8,128)(2,1)}, bf16[128,1024]{1,0:T(8,128)(2,1)S(1)}, u32[]{:S(2)}, u32[]{:S(2)}) collective-permute-start(bf16[128,1024]{1,0:T(8,128)(2,1)} %collective-permute-done.15), channel_id=1, source_target_pairs={{220,252},{92,124},{221,253},{93,125},{222,254},{94,126},{223,255}... | collective-permute-start | bytes 786440 | tf_op jit(solution)/shard_map/ppermute | solution.py:446
  116.9 1.0 copy-start.1
  117.9 0.9 copy-start.3
  118.8 0.9 copy-start.5
  119.8 0.9 copy-start.7
  120.7 0.9 copy-start.9
  125.3 8.4 %copy-start.13 = (bf16[128,1024]{1,0:T(8,128)(2,1)S(1)}, bf16[128,1024]{1,0:T(8,128)(2,1)}, u32[]{:S(2)}) copy-start(bf16[128,1024]{1,0:T(8,128)(2,1)} %copy-done.12) | copy-start | bytes 786436
  129.0 26.1 %collective-permute-start.25 = (bf16[256,2048]{1,0:T(8,128)(2,1)S(1)}, bf16[256,2048]{1,0:T(8,128)(2,1)S(1)}, u32[]{:S(2)}, u32[]{:S(2)}) collective-permute-start(bf16[256,2048]{1,0:T(8,128)(2,1)S(1)} %grad_other.3), channel_id=1, source_target_pairs={{0,2},{1,3},{2,0},{3,1},{4,6},{5,7},{6,4},{7,5},{8,10},{9,11},{10,... | collective-permute-start | bytes 3145736 | tf_op jit(solution)/shard_map/ppermute | solution.py:455
  129.6 46.0 %collective-permute-start.24 = (bf16[256,2048]{1,0:T(8,128)(2,1)S(1)}, bf16[256,2048]{1,0:T(8,128)(2,1)S(1)}, u32[]{:S(2)}, u32[]{:S(2)}) collective-permute-start(bf16[256,2048]{1,0:T(8,128)(2,1)S(1)} %grad_other.2), channel_id=1, source_target_pairs={{0,2},{1,3},{2,0},{3,1},{4,6},{5,7},{6,4},{7,5},{8,10},{9,11},{10,... | collective-permute-start | bytes 3145736 | tf_op jit(solution)/shard_map/ppermute | solution.py:455
  131.2 11.1 %collective-permute-start.6 = (bf16[128,1024]{1,0:T(8,128)(2,1)S(1)}, bf16[128,1024]{1,0:T(8,128)(2,1)S(1)}, u32[]{:S(2)}, u32[]{:S(2)}) collective-permute-start(bf16[128,1024]{1,0:T(8,128)(2,1)S(1)} %subtract_convert_fusion), channel_id=1, source_target_pairs={{4,0},{8,4},{12,8},{16,12},{20,16},{24,20},{28,24},{32,28},{36,32}... | collective-permute-start | bytes 786440 | tf_op jit(solution)/shard_map/ppermute | solution.py:445
  133.7 11.6 %collective-permute-start.7 = (bf16[128,1024]{1,0:T(8,128)(2,1)S(1)}, bf16[128,1024]{1,0:T(8,128)(2,1)S(1)}, u32[]{:S(2)}, u32[]{:S(2)}) collective-permute-start(bf16[128,1024]{1,0:T(8,128)(2,1)S(1)} %copy-done.13), channel_id=1, source_target_pairs={{0,252},{4,0},{8,4},{12,8},{16,12},{20,16},{24,20},{28,24},{32,28}... | collective-permute-start | bytes 786440 | tf_op jit(solution)/shard_map/ppermute | solution.py:436
  133.8 8.4 %collective-permute-start.5 = (bf16[128,1024]{1,0:T(8,128)(2,1)S(1)}, bf16[128,1024]{1,0:T(8,128)(2,1)S(1)}, u32[]{:S(2)}, u32[]{:S(2)}) collective-permute-start(bf16[128,1024]{1,0:T(8,128)(2,1)S(1)} %collective-permute-done.4), channel_id=1, source_target_pairs={{188,252},{60,124},{189,253},{61,125},{190,254},{62,126},{191,255}... | collective-permute-start | bytes 786440 | tf_op jit(solution)/shard_map/ppermute | solution.py:446
